TPU v7x, 512 devices: a whole 4x8x8 slice. The times are simulated.
512 devices in a mesh: row: 16 (over z, core), col: 32 (over x, y).
Axes of the slice: x: 4, y: 8, z: 8, core: 2. Of those that a mesh axis runs over, the one named last changes fastest.
Arguments:
- profiles: bfloat16 [50, 65536], P(None, ('col', 'row')), may hold values from -1.1953125 to 1.1953125
- cell_width: bfloat16 [65536], P(('col', 'row')), may hold values from 1 to 3
- basis: bfloat16 [64, 65536], P(None, ('col', 'row')), may hold values from -6 to 6
- block_lists: int32 [16, 32, 2, 128], P('row', 'col'), may hold values from 0 to 31, as said below
- block_counts: int32 [16, 32], P('row', 'col'), may hold values from 8 to 128, as said below
- landmarks: int32 [32], replicated, may hold values from 0 to 511, as said below
Outputs:
- row_scaling: float32 [65536], P('row')
- column_scaling: float32 [65536], P('col')
- ritz_basis: float32 [64, 65536], P(None, ('row', 'col'))
Inputs may be any that keep to these rules, and one draw needn't show every extreme that they name: `block_lists`: in each tile the first block_counts slots name distinct blocks, row block below 32 and column block below 16; every block of the tile whose global row block and global column block differ by at most one is among them; later slots also name blocks of the tile. `block_counts`: A tile whose column cells lie among its own row cells has exactly 128 live slots. `landmarks`: Distinct, increasing, one in each aligned group of 16 consecutive blocks.
All inputs are finite; a program needn't handle non-finite values.
Results may differ from a plain program's by a relative error of at most 0.0057.
Values may be sent and summed in bfloat16 or wider, within the bound.
A program may use at most 64 MiB of HBM per device.

v0:
```python
import jax
import jax.numpy as jnp
from jax import lax
from jax.sharding import PartitionSpec as P

BLK = 128
PCS = 50
COLS = 64
SWEEPS = 3


affinity_scale = 0.001953125
highest = lax.Precision.HIGHEST


def block_kernel(row_slots, col_slots, live_mask, geometry):
    row_prof, row_norm, row_width, col_prof, col_norm, col_width = geometry
    left_prof = jnp.take(row_prof, row_slots, axis=1)
    right_prof = jnp.take(col_prof, col_slots, axis=1)
    inner_product = jnp.einsum(
        "pkb,pkd->kbd", left_prof, right_prof, preferred_element_type=jnp.float32
    )
    distance = (
        jnp.take(row_norm, row_slots, axis=0)[:, :, None]
        + jnp.take(col_norm, col_slots, axis=0)[:, None, :]
        - 2.0 * inner_product
    )
    width_pair = (
        jnp.take(row_width, row_slots, axis=0)[:, :, None]
        * jnp.take(col_width, col_slots, axis=0)[:, None, :]
    )
    return jnp.exp(-distance / width_pair) * (affinity_scale * live_mask)[:, None, None]


def affinity_sweep(update, initial, slot_lists, block_total, geometry):
    group_size = 8
    row_blocks = geometry[1].shape[0]
    col_blocks = geometry[4].shape[0]

    def advance(number, totals):
        first_slot = number * group_size
        row_slots = lax.dynamic_slice_in_dim(slot_lists[0], first_slot, group_size)
        col_slots = lax.dynamic_slice_in_dim(slot_lists[1], first_slot, group_size)
        live_mask = (first_slot + jnp.arange(group_size) < block_total).astype(jnp.float32)
        kernel = block_kernel(row_slots, col_slots, live_mask, geometry)
        row_onehot = (row_slots[:, None] == jnp.arange(row_blocks)[None, :]).astype(jnp.float32)
        col_onehot = (col_slots[:, None] == jnp.arange(col_blocks)[None, :]).astype(jnp.float32)
        return update(totals, kernel, row_slots, col_slots, row_onehot, col_onehot)

    trip_count = (block_total + group_size - 1) // group_size
    return lax.fori_loop(0, trip_count, advance, initial)


def with_rows(col_scaling):

    def update(totals, kernel, row_slots, col_slots, row_onehot, col_onehot):
        picked = jnp.take(col_scaling, col_slots, axis=0)
        partial_value = jnp.einsum("kbd,kd->kb", kernel, picked, precision=highest)
        return totals + jnp.einsum("kr,kb->rb", row_onehot, partial_value, precision=highest)

    return update


def with_cols(row_scaling):

    def update(totals, kernel, row_slots, col_slots, row_onehot, col_onehot):
        picked = jnp.take(row_scaling, row_slots, axis=0)
        partial_value = jnp.einsum("kbd,kb->kd", kernel, picked, precision=highest)
        return totals + jnp.einsum("kc,kd->cd", col_onehot, partial_value, precision=highest)

    return update


def with_subspace(scaled_basis):

    def update(totals, kernel, row_slots, col_slots, row_onehot, col_onehot):
        picked = jnp.take(scaled_basis, col_slots, axis=1)
        partial_value = jnp.einsum(
            "ckd,kbd->ckb", picked, kernel.astype(jnp.bfloat16), preferred_element_type=jnp.float32
        )
        return totals + jnp.einsum("kr,ckb->crb", row_onehot, partial_value, precision=highest)

    return update


def column_reciprocal(partial_value):
    return 1.0 / lax.psum(partial_value, "row")


def row_reciprocal(partial_value):
    return 1.0 / lax.psum(partial_value, "col")


def body(profiles, cell_width, basis, block_lists, block_counts, landmarks):
    col_prof, col_bw, col_basis = (
        lax.all_gather(profiles, "row", axis=1, tiled=True),
        lax.all_gather(cell_width, "row", axis=0, tiled=True),
        lax.all_gather(basis, "row", axis=1, tiled=True),
    )
    share_ratio = lax.axis_size("col") // lax.axis_size("row")
    cells_col = col_prof.shape[1]
    cells_row = cells_col * share_ratio
    every_prof, every_bw = (
        lax.all_gather(col_prof, "col", axis=1, tiled=True),
        lax.all_gather(col_bw, "col", axis=0, tiled=True),
    )
    first_cell = lax.axis_index("row") * cells_row
    row_prof = lax.dynamic_slice_in_dim(every_prof, first_cell, cells_row, 1)
    row_bw = lax.dynamic_slice_in_dim(every_bw, first_cell, cells_row, 0)
    row_blocks = cells_row // BLK
    col_blocks = cells_col // BLK
    geometry = (
        row_prof.reshape(PCS, row_blocks, BLK),
        jnp.sum(jnp.square(row_prof.astype(jnp.float32)), axis=0).reshape(row_blocks, BLK),
        row_bw.astype(jnp.float32).reshape(row_blocks, BLK),
        col_prof.reshape(PCS, col_blocks, BLK),
        jnp.sum(jnp.square(col_prof.astype(jnp.float32)), axis=0).reshape(col_blocks, BLK),
        col_bw.astype(jnp.float32).reshape(col_blocks, BLK),
    )
    slot_lists = block_lists[0, 0]
    block_total = block_counts[0, 0]
    row_scaling = jnp.ones((row_blocks, BLK), jnp.float32)
    col_scaling = jnp.ones((col_blocks, BLK), jnp.float32)
    for sweep_number in range(SWEEPS):
        col_part = affinity_sweep(
            with_cols(row_scaling),
            jnp.zeros((col_blocks, BLK), jnp.float32),
            slot_lists,
            block_total,
            geometry,
        )
        col_scaling = column_reciprocal(col_part.reshape(-1)).reshape(col_blocks, BLK)
        if sweep_number < SWEEPS - 1:
            row_part = affinity_sweep(
                with_rows(col_scaling),
                jnp.zeros((row_blocks, BLK), jnp.float32),
                slot_lists,
                block_total,
                geometry,
            )
            row_scaling = row_reciprocal(row_part.reshape(-1)).reshape(row_blocks, BLK)
    scaled_basis = (col_basis.astype(jnp.float32) * col_scaling.reshape(-1)[None, :]).astype(
        jnp.bfloat16
    )
    scaled_basis = scaled_basis.reshape(COLS, col_blocks, BLK)
    empty_sums = jnp.zeros((COLS, row_blocks, BLK), jnp.float32)
    row_part = affinity_sweep(
        with_rows(col_scaling),
        jnp.zeros((row_blocks, BLK), jnp.float32),
        slot_lists,
        block_total,
        geometry,
    )
    row_flat = row_reciprocal(row_part.reshape(-1))
    mixed_sums = affinity_sweep(
        with_subspace(scaled_basis), empty_sums, slot_lists, block_total, geometry
    )
    share_cols = lax.psum_scatter(
        mixed_sums.reshape(COLS, cells_row), "col", scatter_dimension=1, tiled=True
    )
    share_width = share_cols.shape[1]
    own_scaling = lax.dynamic_slice_in_dim(
        row_flat, lax.axis_index("col") * share_width, share_width
    )
    projected = share_cols * own_scaling[None, :]
    shard_number = lax.axis_index("row") * lax.axis_size("col") + lax.axis_index("col")
    cell_ids = shard_number * share_width + jnp.arange(share_width)
    block_ids = cell_ids // BLK
    cell_mask = jnp.any(block_ids[:, None] == landmarks[None, :], axis=1).astype(jnp.float32)
    masked = projected * cell_mask[None, :]
    gram_local = jnp.dot(masked, masked.T, precision=highest)
    gram_matrix = lax.psum(gram_local, ("row", "col")) / (landmarks.shape[0] * BLK)
    lower_factor = jnp.linalg.cholesky(gram_matrix)
    ritz_basis = jax.scipy.linalg.solve_triangular(lower_factor, projected, lower=True)
    return (row_flat, col_scaling.reshape(-1), ritz_basis)


def solution(mesh):
    placed = (
        P(None, ("col", "row")),
        P(("col", "row")),
        P(None, ("col", "row")),
        P("row", "col", None, None),
        P("row", "col"),
        P(),
    )
    return jax.shard_map(
        body,
        mesh=mesh,
        in_specs=placed,
        out_specs=(P("row"), P("col"), P(None, ("row", "col"))),
        check_vma=False,
    )
```

profile of v0, /device:TPU:1, one launch (start us, length us, event | category | flops | bytes accessed | tf_op | source)
XLA Modules:
  0.0 1562.6 jit_solution(1949807725470026246)
XLA Ops:
  7.2 26.7 %all_gather.15 = bf16[50,2048]{1,0:T(8,128)(2,1)} all-gather(bf16[50,128]{1,0:T(8,128)(2,1)} %param.28), channel_id=1, replica_groups=mesh['row'=16,'col'=32] {'row'}, dimensions={1}, use_global_device_ids=true | all-gather | bytes 217600 | tf_op jit(solution)/shard_map/all_gather | solution.py:96
  34.7 1.0 copy.82
  35.8 14.6 all-gather
  51.2 33.5 %all_gather.18 = bf16[65536]{0:T(1024)(128)(2,1)S(1)} all-gather(bf16[2048]{0:T(1024)(128)(2,1)S(1)} %bitcast.327), channel_id=1, replica_groups=mesh['row'=16,'col'=32] {'col'}, dimensions={0}, use_global_device_ids=true | all-gather | bytes 135168 | tf_op jit(solution)/shard_map/all_gather | solution.py:105
  84.8 23.6 %all_gather.19 = bf16[64,2048]{1,0:T(8,128)(2,1)S(1)} all-gather(bf16[64,128]{1,0:T(8,128)(2,1)} %param.30), channel_id=1, replica_groups=mesh['row'=16,'col'=32] {'row'}, dimensions={1}, use_global_device_ids=true | all-gather | bytes 278528 | tf_op jit(solution)/shard_map/all_gather | solution.py:98
  108.3 1.0 multiply_reduce_fusion.1
  109.3 18.9 %all-gather.3.cloned.1.call-done = bf16[50,65536]{1,0:T(8,128)(2,1)} async-done(((bf16[50,2048]{1,0:T(8,128)(2,1)}), bf16[50,65536]{1,0:T(8,128)(2,1)}) %all-gather.3.cloned.1.call-update) | async-done | bytes 6553616 | tf_op jit(solution)/shard_map/all_gather | solution.py:104
  128.3 1.1 multiply_reduce_fusion
  129.7 14.5 while.70
  135.4 0.8 fusion.235
  137.0 0.8 fusion.234
  142.6 0.8 fusion.235
  144.2 125.7 %psum.49 = f32[2048]{0:T(1024)S(1)} all-reduce(f32[2048]{0:T(1024)S(1)} %bitcast.328), channel_id=1, replica_groups=mesh['row'=16,'col'=32] {'row'}, use_global_device_ids=true, to_apply=%region_4.9 | all-reduce | flops 2048 | bytes 16384 | tf_op jit(solution)/shard_map/psum | solution.py:87
  270.0 15.3 while.71
  275.6 0.8 fusion.243
  276.4 0.9 fusion.244
  283.2 0.8 fusion.243
  284.0 0.9 fusion.244
  285.2 210.8 %psum.50 = f32[4096]{0:T(1024)S(1)} all-reduce(f32[4096]{0:T(1024)S(1)} %bitcast.325), channel_id=1, replica_groups=mesh['row'=16,'col'=32] {'col'}, use_global_device_ids=true, to_apply=%region_7.12 | all-reduce | flops 4096 | bytes 32768 | tf_op jit(solution)/shard_map/psum | solution.py:91
  496.0 14.4 while.72
  501.6 0.8 fusion.251
  503.2 0.8 fusion.250
  508.8 0.8 fusion.251
  510.4 159.7 %psum.51 = f32[2048]{0:T(1024)S(1)} all-reduce(f32[2048]{0:T(1024)S(1)} %bitcast.329), channel_id=1, replica_groups=mesh['row'=16,'col'=32] {'row'}, use_global_device_ids=true, to_apply=%region_10.15 | all-reduce | flops 2048 | bytes 16384 | tf_op jit(solution)/shard_map/psum | solution.py:87
  670.2 15.3 while.73
  676.6 0.9 fusion.260
  683.5 0.8 fusion.259
  684.2 0.9 fusion.260
  685.5 172.4 %psum.52 = f32[4096]{0:T(1024)S(1)} all-reduce(f32[4096]{0:T(1024)S(1)} %bitcast.326), channel_id=1, replica_groups=mesh['row'=16,'col'=32] {'col'}, use_global_device_ids=true, to_apply=%region_13.18 | all-reduce | flops 4096 | bytes 32768 | tf_op jit(solution)/shard_map/psum | solution.py:91
  857.8 14.4 while.74
  863.5 0.8 fusion.267
  865.1 0.8 fusion.266
  870.7 0.8 fusion.267
  872.3 197.1 %psum.53 = f32[2048]{0:T(1024)S(1)} all-reduce(f32[2048]{0:T(1024)S(1)} %bitcast.330), channel_id=1, replica_groups=mesh['row'=16,'col'=32] {'row'}, use_global_device_ids=true, to_apply=%region_16.21 | all-reduce | flops 2048 | bytes 16384 | tf_op jit(solution)/shard_map/psum | solution.py:87
  1070.0 14.6 while.76
  1076.4 0.9 fusion.285
  1083.7 0.9 fusion.285
  1084.6 1.6 copy.88
  1086.3 15.4 while.75
  1092.9 0.9 fusion.276
  1100.5 0.9 fusion.276
  1101.7 237.0 %psum.54 = f32[4096]{0:T(1024)S(1)} all-reduce(f32[4096]{0:T(1024)S(1)} %bitcast.324), channel_id=1, replica_groups=mesh['row'=16,'col'=32] {'col'}, use_global_device_ids=true, to_apply=%region_19.24 | all-reduce | flops 4096 | bytes 32768 | tf_op jit(solution)/shard_map/psum | solution.py:91
  1338.8 55.0 %reduce-scatter.2.cloned.1.call-done = f32[64,128]{1,0:T(8,128)} async-done(((f32[64,4096]{1,0:T(8,128)}), f32[64,128]{1,0:T(8,128)}) %reduce-scatter.2.cloned.1.call-update) | async-done | bytes 32784 | tf_op jit(solution)/shard_map/reduce_scatter | solution.py:158
  1393.8 1.0 fusion.132
  1394.9 147.1 %psum.55 = f32[64,64]{0,1:T(8,128)S(1)} all-reduce(f32[64,64]{0,1:T(8,128)S(1)} %fusion.132), channel_id=1, replica_groups=mesh['row'=16,'col'=32] {'row','col'}, use_global_device_ids=true, to_apply=%region_24.29 | all-reduce | flops 4096 | bytes 32768 | tf_op jit(solution)/shard_map/psum | solution.py:172
  1542.1 5.8 cholesky.16
  1549.3 4.9 custom-call.7
  1554.2 1.6 fusion.129
  (277 shorter events, 89.6 us)
Async XLA Ops:
  7.2 121.1 %all-gather.3.cloned.1.call-start = ((), (), s32[]{:S(2)}) async-start(), calls=%async_computation.1 | async-start | bytes 7569408 | tf_op jit(solution)/shard_map/all_gather | solution.py:104
  34.0 1359.8 %reduce-scatter.2.cloned.1.call-start = ((), (), s32[]{:S(2)}) async-start(), calls=%async_computation.2 | async-start | bytes 1081344 | tf_op jit(solution)/shard_map/reduce_scatter | solution.py:158
  1069.4 0.6 copy-start
  1338.7 217.1 %copy-start.1 = (f32[4096]{0:T(1024)}, f32[4096]{0:T(1024)S(1)}, u32[]{:S(2)}) copy-start(f32[4096]{0:T(1024)S(1)} %broadcast_divide_fusion) | copy-start | bytes 49156
Sparse Core Ops, SparseCore 0:
  34.1 94.1 all-gather.2
  1086.4 307.4 reduce-scatter.1
where the time goes:
time: 1570 us; the launch traced here: 1560 us
  blocking collectives  1350 us (86%)
  waiting for transfers between devices  74 us (5%)
  local copies, waits for them, and re-layouts  69.2 us (4%)
  other arithmetic  27.8 us (2%)
  matrix products  27 us (2%)
    psum x3, blocking collectives, row_reciprocal(): return 1.0 / lax.psum(partial_value, 'col')  620 us
    psum x3, blocking collectives, column_reciprocal(): return 1.0 / lax.psum(partial_value, 'row')  483 us
    psum x1, blocking collectives, body(): lax.psum(gram_local, ('row', 'col')) / (landmarks.shape[0] * BLK)  147 us
    reduce_scatter x1, waiting for transfers between devices, body(): lax.psum_scatter(mixed_sums.reshape(COLS, cells_row), 'col', scatter_dime...  55 us
    all_gather x1, blocking collectives, body(): lax.all_gather(col_bw, 'col', axis=0, tiled=True)  33.5 us
  transfers between devices with their start and end apart: 2, of which 2 were waited for; matrix products, arithmetic and copies ran while one was open for 1% of the time, Pallas kernels for 0%

commit v1 on v0

v1 whole, which is shorter than its diff:
```python
import functools

import jax
import jax.numpy as jnp
from jax import lax
from jax.experimental import pallas as pl
from jax.experimental.pallas import tpu as pltpu
from jax.sharding import PartitionSpec as P

BLK = 128
PCS = 50
COLS = 64
SWEEPS = 3
KDIM = 64
CP = 16
RP = 32
SCALE = 512.0
MESH = pl.DeviceIdType.MESH
highest = lax.Precision.HIGHEST
f32 = jnp.float32
bf16 = jnp.bfloat16

ROW, COL, ROWKEY, COLKEY, KEEP, LAST, HAS, MARK = range(8)


def slot_table(slot_lists, count, landmarks, own_block, row_blocks):
    slots = slot_lists.shape[1]
    number = jnp.arange(slots, dtype=jnp.int32)
    live = number < count
    row = slot_lists[0]
    col = slot_lists[1]
    key = jnp.where(live, row, RP) * slots + number
    rank = jnp.sum((key[None, :] < key[:, None]).astype(jnp.int32), axis=1)
    place = (rank[None, :] == number[:, None]).astype(jnp.int32)
    pick = lambda v: jnp.sum(place * v[None, :], axis=1)
    rows, cols, lives = pick(row), pick(col), pick(live.astype(jnp.int32))
    rowkey = jnp.where(lives > 0, rows, RP)
    colkey = jnp.where(lives > 0, cols, CP)
    before = jnp.concatenate([jnp.full((1,), -1, jnp.int32), rowkey[:-1]])
    keep = (before == rowkey).astype(jnp.int32)
    upto = jnp.sum((rowkey[None, :] <= number[:, None]).astype(jnp.int32), axis=1)
    has = jnp.any(rowkey[None, :] == number[:, None], axis=1).astype(jnp.int32)
    last = jnp.clip(upto - 1, 0, slots - 1)
    mark = jnp.broadcast_to(jnp.any(landmarks == own_block).astype(jnp.int32), (slots,))
    return jnp.stack([rows, cols, rowkey, colkey, keep, last, has, mark])


def tile_kernel(
    dims,
    prof_ref,
    width_ref,
    basis_ref,
    idx,
    gram_ref,
    proj_ref,
    rows_ref,
    cols_ref,
    msg32,
    rowout,
    colbuf,
    basisbuf,
    rowbuf,
    left,
    uleft,
    uright,
    hot16,
    hot32,
    rhi,
    rlo,
    chi,
    clo,
    sbas,
    aff,
    sums,
    share,
    zvec,
    xvec,
    yvec,
    xshare,
    yshare,
    xgram,
    ygram,
    zgram,
    send_sem,
    recv_sem,
):
    NR, NC, NX, NY, slots = dims
    me_r = lax.axis_index("row")
    me_c = lax.axis_index("col")
    me_x = me_c // NY
    me_y = me_c % NY
    to_r = me_c // 2
    to_c = (me_c % 2) * NR + me_r
    from_c = 2 * me_r + me_c // NR
    from_r = me_c % NR
    moves = (to_r != me_r) | (to_c != me_c)

    def zdev(d):
        return (lax.rem(me_r + d, NR), me_c)

    def xdev(d):
        return (me_r, lax.rem(me_x + d, NX) * NY + me_y)

    def ydev(d):
        return (me_r, me_x * NY + lax.rem(me_y + d, NY))

    groups = {"z": (NR, zdev), "x": (NX, xdev), "y": (NY, ydev)}
    sent = []

    def push(axis, src_of, dst, number):
        size, device = groups[axis]
        for d in range(1, size):
            pltpu.make_async_remote_copy(
                src_ref=src_of(d),
                dst_ref=dst.at[d],
                send_sem=send_sem.at[number],
                recv_sem=recv_sem.at[number],
                device_id=device(d),
                device_id_type=MESH,
            ).start()
        region = dst.at[pl.ds(1, size - 1)]
        sent.append((region, number))
        return lambda: pltpu.make_async_copy(region, region, recv_sem.at[number]).wait()

    prof = prof_ref[...].astype(f32)
    half = jnp.sum(prof * prof, axis=0, keepdims=True) * -0.5
    h1 = half.astype(bf16).astype(f32)
    h2 = (half - h1).astype(bf16).astype(f32)
    h3 = half - h1 - h2
    width = width_ref[...].astype(f32)
    ones = jnp.ones((1, BLK), f32)
    msg32[...] = jnp.zeros_like(msg32)
    for side in range(2):
        msg32[side, 0:PCS, :] = prof
        a, b = (50, 53) if side == 0 else (53, 50)
        msg32[side, a : a + 1, :] = h1
        msg32[side, a + 1 : a + 2, :] = h2
        msg32[side, a + 2 : a + 3, :] = h3
        for n in range(3):
            msg32[side, b + n : b + n + 1, :] = ones
        w = 56 + side
        msg32[side, w : w + 1, :] = width
    colbuf[0] = msg32[1].astype(bf16)
    basisbuf[0] = basis_ref[...]
    outgoing = rowout.at[0]
    rowout[0] = msg32[0].astype(bf16)

    barrier = pltpu.get_barrier_semaphore()
    for size, device in groups.values():
        for d in range(1, size):
            pl.semaphore_signal(barrier, inc=1, device_id=device(d), device_id_type=MESH)

    @pl.when(moves)
    def _():
        pl.semaphore_signal(barrier, inc=1, device_id=(to_r, to_c), device_id_type=MESH)
        pl.semaphore_signal(barrier, inc=1, device_id=(from_r, from_c), device_id_type=MESH)

    near = NR + NX + NY - 3

    it16 = lax.broadcasted_iota(jnp.int32, (CP, BLK), 0)
    it32 = lax.broadcasted_iota(jnp.int32, (RP, BLK), 0)

    def tables(k, carry):
        hot32[k] = (it32 == k).astype(f32).astype(bf16)
        return carry

    lax.fori_loop(0, RP + 1, tables, 0)

    def tables16(k, carry):
        hot16[k] = (it16 == k).astype(f32).astype(bf16)
        return carry

    lax.fori_loop(0, CP + 1, tables16, 0)

    pl.semaphore_wait(barrier, near + 2 * moves.astype(jnp.int32))

    move = pltpu.make_async_remote_copy(
        src_ref=outgoing,
        dst_ref=rowbuf.at[0],
        send_sem=send_sem.at[0],
        recv_sem=recv_sem.at[0],
        device_id=(to_r, to_c),
        device_id_type=MESH,
    )
    stay = pltpu.make_async_copy(outgoing, rowbuf.at[0], recv_sem.at[0])

    @pl.when(moves)
    def _():
        move.start()

    @pl.when(jnp.logical_not(moves))
    def _():
        stay.start()

    wait_col = push("z", lambda d: colbuf.at[0], colbuf, 1)

    @pl.when(moves)
    def _():
        move.wait_recv()
        move.wait_send()

    @pl.when(jnp.logical_not(moves))
    def _():
        stay.wait()

    for d in range(1, NX):
        pltpu.make_async_remote_copy(
            src_ref=rowbuf.at[0],
            dst_ref=rowbuf.at[d],
            send_sem=send_sem.at[2],
            recv_sem=recv_sem.at[2],
            device_id=xdev(d),
            device_id_type=MESH,
        ).start()
    region = rowbuf.at[pl.ds(1, NX - 1)]
    sent.append((region, 2))
    pltpu.make_async_copy(region, region, recv_sem.at[2]).wait()
    for d in range(1, NY):
        pltpu.make_async_remote_copy(
            src_ref=rowbuf.at[pl.ds(0, NX)],
            dst_ref=rowbuf.at[pl.ds(d * NX, NX)],
            send_sem=send_sem.at[3],
            recv_sem=recv_sem.at[3],
            device_id=ydev(d),
            device_id_type=MESH,
        ).start()
    region_y = rowbuf.at[pl.ds(NX, (NY - 1) * NX)]
    sent.append((region_y, 3))

    wait_basis = push("z", lambda d: basisbuf.at[0], basisbuf, 4)
    wait_col()

    def col_place(j):
        return lax.rem(me_r - j + NR, NR)

    def row_place(i):
        return lax.rem(me_y - lax.rem(i, NY) + NY, NY) * NX + lax.rem(me_x - i // NY + NX, NX)

    def col_prepare(n, carry):
        turned = colbuf[n].astype(f32).T
        left[n] = turned.astype(bf16)
        w = jnp.broadcast_to(turned[:, 57:58], (BLK, BLK))
        uleft[n] = (2.0 * 1.4426950408889634) / w
        return carry

    lax.fori_loop(0, NR, col_prepare, 0)

    pltpu.make_async_copy(region_y, region_y, recv_sem.at[3]).wait()

    def row_prepare(n, carry):
        w = rowbuf[n].astype(f32)[56:57, :]
        uright[n] = jnp.broadcast_to(1.0 / w, (8, BLK))
        return carry

    lax.fori_loop(0, NC, row_prepare, 0)

    def build(s, carry):
        j = col_place(idx[COL, s])
        i = row_place(idx[ROW, s])
        d = jnp.dot(left[j], rowbuf[i], preferred_element_type=f32)
        e = d * uleft[j] * uright[i][0:1, :]
        aff[s] = jnp.exp2(e).astype(bf16)
        return carry

    lax.fori_loop(0, slots, build, 0, unroll=4)

    def col_pass():
        def step(s, acc):
            i = idx[ROW, s]
            hot = hot16[idx[COLKEY, s]]
            lhs = jnp.concatenate([rhi[i] * hot, rlo[i] * hot], axis=0)
            return acc + lax.dot_general(
                lhs, aff[s], (((1,), (1,)), ((), ())), preferred_element_type=f32
            )

        acc = lax.fori_loop(0, slots, step, jnp.zeros((2 * CP, BLK), f32), unroll=4)
        return acc[0:CP] + acc[CP:]

    def row_pass():
        def step(s, acc):
            j = idx[COL, s]
            hot = hot32[idx[ROWKEY, s]]
            lhs = jnp.concatenate([chi[j] * hot, clo[j] * hot], axis=0)
            return acc + jnp.dot(lhs, aff[s], preferred_element_type=f32)

        acc = lax.fori_loop(0, slots, step, jnp.zeros((2 * RP, BLK), f32), unroll=4)
        return acc[0:RP] + acc[RP:]

    def col_total(k, part):
        buf = zvec.at[k]
        buf[0] = part
        wait = push("z", lambda d: buf.at[0], buf, 5 + k)
        wait()
        total = buf[lax.rem(me_r, NR)]
        for r in range(1, NR):
            total = total + buf[lax.rem(me_r - r + NR, NR)]
        return total

    def row_total(k, part, during=None):
        bx = xvec.at[k]
        bx[0] = part
        wait = push("x", lambda d: bx.at[0], bx, 8 + k)
        if during is not None:
            during()
        wait()
        total = bx[me_x]
        for x in range(1, NX):
            total = total + bx[lax.rem(me_x - x + NX, NX)]
        by = yvec.at[k]
        by[0] = total
        push("y", lambda d: by.at[0], by, 11 + k)()
        total = by[me_y]
        for y in range(1, NY):
            total = total + by[lax.rem(me_y - y + NY, NY)]
        return total

    def spread(vec, blocks, width_, hi_ref, lo_ref):
        for n in range(blocks):
            v = jnp.broadcast_to(vec[n : n + 1, :], (width_, BLK))
            hi = v.astype(bf16)
            hi_ref[n] = hi
            lo_ref[n] = (v - hi.astype(f32)).astype(bf16)

    rhi[...] = jnp.ones_like(rhi)
    rlo[...] = jnp.zeros_like(rlo)
    for k in range(SWEEPS):
        cvec = SCALE / col_total(k, col_pass())
        spread(cvec, NR, RP, chi, clo)
        if k < SWEEPS - 1:
            rvec = SCALE / row_total(k, row_pass())
            spread(rvec, NC, CP, rhi, rlo)
    cols_ref[...] = cvec

    wait_basis()
    for j in range(NR):
        block = basisbuf[col_place(j)].astype(f32) * cvec[j : j + 1, :]
        sbas[j] = block.astype(bf16)

    def subspace():
        def step(s, acc):
            keep = idx[KEEP, s].astype(f32)
            acc = acc * keep + jnp.dot(sbas[idx[COL, s]], aff[s], preferred_element_type=f32)
            sums[s] = acc
            return acc

        lax.fori_loop(0, slots, step, jnp.zeros((COLS, BLK), f32), unroll=4)

        def pick(i, carry):
            share[i] = sums[idx[LAST, i]] * idx[HAS, i].astype(f32)
            return carry

        lax.fori_loop(0, NC, pick, 0)

    rvec = SCALE / row_total(SWEEPS - 1, row_pass(), subspace)
    rows_ref[...] = rvec

    def own_part(x):
        return share.at[pl.ds(x * NY, NY)]

    wait = push("x", lambda d: own_part(lax.rem(me_x + d, NX)), xshare, 14)
    wait()

    def add_x(n, carry):
        total = jnp.zeros((COLS, BLK), f32) + share[me_x * NY + n]
        for d in range(1, NX):
            total = total + xshare[d, n]
        xshare[0, n] = total
        return carry

    lax.fori_loop(0, NY, add_x, 0)
    wait = push("y", lambda d: xshare.at[0, lax.rem(me_y + d, NY)], yshare, 15)
    wait()
    total = xshare[0, me_y]
    for d in range(1, NY):
        total = total + yshare[d]
    proj = total * (rows_ref[pl.ds(me_c, 1), :] * (1.0 / SCALE))
    proj_ref[...] = proj

    masked = proj * idx[MARK, 0].astype(f32)
    gram = lax.dot_general(
        masked, masked, (((1,), (1,)), ((), ())), precision=highest, preferred_element_type=f32
    )
    half_rows = COLS // 2
    packed = jnp.concatenate([gram[:half_rows], gram[half_rows:]], axis=1)
    for axis, buf, number, size, me in (
        ("x", xgram, 16, NX, me_x),
        ("y", ygram, 17, NY, me_y),
        ("z", zgram, 18, NR, me_r),
    ):
        buf[0] = packed
        push(axis, lambda d, buf=buf: buf.at[0], buf, number)()
        packed = buf[me]
        for n in range(1, size):
            packed = packed + buf[lax.rem(me - n + size, size)]
    gram_ref[...] = packed

    for region, number in sent:
        pltpu.make_async_copy(region, region, send_sem.at[number]).wait()


def finish_kernel(gram_ref, proj_ref, rows_in, cols_in, ritz_ref, rows_ref, cols_ref, *, cells):
    rows_ref[...] = rows_in[...]
    cols_ref[...] = cols_in[...]
    half_rows = COLS // 2
    packed = gram_ref[...] * (1.0 / cells)
    gram = jnp.concatenate([packed[:, :COLS], packed[:, COLS:]], axis=0)
    proj = proj_ref[...]
    number = lax.broadcasted_iota(jnp.int32, (COLS, 1), 0)
    for k in range(COLS):
        scale = 1.0 / jnp.sqrt(gram[k : k + 1, k : k + 1])
        grow = gram[k : k + 1, :] * scale
        prow = proj[k : k + 1, :] * scale
        ritz_ref[k : k + 1, :] = prow
        factor = jnp.where(number > k, gram[:, k : k + 1] * scale, 0.0)
        gram = gram - factor * grow
        proj = proj - factor * prow


def body(mesh_sizes, profiles, cell_width, basis, block_lists, block_counts, landmarks):
    NR, NC, NX, NY = mesh_sizes
    slots = block_lists.shape[-1]
    own_block = lax.axis_index("row") * NC + lax.axis_index("col")
    table = slot_table(block_lists[0, 0], block_counts[0, 0], landmarks, own_block, NC)
    vmem = pl.BlockSpec(memory_space=pltpu.VMEM)
    smem = pl.BlockSpec(memory_space=pltpu.SMEM)
    half_rows = COLS // 2
    gram, proj, rows, cols = pl.pallas_call(
        functools.partial(tile_kernel, (NR, NC, NX, NY, slots)),
        out_shape=(
            jax.ShapeDtypeStruct((half_rows, BLK), f32),
            jax.ShapeDtypeStruct((COLS, BLK), f32),
            jax.ShapeDtypeStruct((RP, BLK), f32),
            jax.ShapeDtypeStruct((CP, BLK), f32),
        ),
        in_specs=[vmem, vmem, vmem, smem],
        out_specs=(vmem,) * 4,
        scratch_shapes=[
            pltpu.VMEM((2, KDIM, BLK), f32),
            pltpu.VMEM((1, KDIM, BLK), bf16),
            pltpu.VMEM((NR, KDIM, BLK), bf16),
            pltpu.VMEM((NR, COLS, BLK), bf16),
            pltpu.VMEM((NC, KDIM, BLK), bf16),
            pltpu.VMEM((NR, BLK, KDIM), bf16),
            pltpu.VMEM((NR, BLK, BLK), f32),
            pltpu.VMEM((NC, 8, BLK), f32),
            pltpu.VMEM((CP + 1, CP, BLK), bf16),
            pltpu.VMEM((RP + 1, RP, BLK), bf16),
            pltpu.VMEM((NC, CP, BLK), bf16),
            pltpu.VMEM((NC, CP, BLK), bf16),
            pltpu.VMEM((NR, RP, BLK), bf16),
            pltpu.VMEM((NR, RP, BLK), bf16),
            pltpu.VMEM((NR, COLS, BLK), bf16),
            pltpu.VMEM((slots, BLK, BLK), bf16),
            pltpu.VMEM((slots, COLS, BLK), f32),
            pltpu.VMEM((NC, COLS, BLK), f32),
            pltpu.VMEM((SWEEPS, NR, CP, BLK), f32),
            pltpu.VMEM((SWEEPS, NX, RP, BLK), f32),
            pltpu.VMEM((SWEEPS, NY, RP, BLK), f32),
            pltpu.VMEM((NX, NY, COLS, BLK), f32),
            pltpu.VMEM((NY, COLS, BLK), f32),
            pltpu.VMEM((NX, half_rows, BLK), f32),
            pltpu.VMEM((NY, half_rows, BLK), f32),
            pltpu.VMEM((NR, half_rows, BLK), f32),
            pltpu.SemaphoreType.DMA((20,)),
            pltpu.SemaphoreType.DMA((20,)),
        ],
        compiler_params=pltpu.CompilerParams(collective_id=0, has_side_effects=True),
        name="tile",
    )(profiles, cell_width.reshape(1, BLK), basis, table)
    ritz, rows, cols = pl.pallas_call(
        functools.partial(finish_kernel, cells=landmarks.shape[0] * BLK),
        out_shape=(
            jax.ShapeDtypeStruct((COLS, BLK), f32),
            jax.ShapeDtypeStruct((RP, BLK), f32),
            jax.ShapeDtypeStruct((CP, BLK), f32),
        ),
        in_specs=[vmem] * 4,
        out_specs=(vmem,) * 3,
        name="finish",
    )(gram, proj, rows, cols)
    return rows[:NC].reshape(-1), cols[:NR].reshape(-1), ritz


def solution(mesh):
    NR, NC = mesh.shape["row"], mesh.shape["col"]
    NX = {32: 4, 4: 2}[NC]
    placed = (
        P(None, ("col", "row")),
        P(("col", "row")),
        P(None, ("col", "row")),
        P("row", "col", None, None),
        P("row", "col"),
        P(),
    )
    return jax.shard_map(
        functools.partial(body, (NR, NC, NX, NC // NX)),
        mesh=mesh,
        in_specs=placed,
        out_specs=(P("row"), P("col"), P(None, ("row", "col"))),
        check_vma=False,
    )
```

time: 1570 us -> 180 us (0.11)
  blocking collectives: 1350 us -> 0 us
  Pallas kernels: 0 us -> 174 us
  waiting for transfers between devices: 74 us -> 0 us
  local copies, waits for them, and re-layouts: 69.2 us -> 1.94 us
  matrix products: 27 us -> 0 us
  other arithmetic: 27.8 us -> 1.28 us
    psum x7 -> x0, blocking collectives: 1250 us -> none  [the longest x3 620 us: row_reciprocal(): return 1.0 / lax.psum(partial_value, 'col')]
    pallas_call x0 -> x2, Pallas kernels: none -> 174 us  [the longest x1 167 us: body(): pl.pallas_call(functools.partial(tile_kernel, (NR, NC, NX, NY, slots)), o...]
    all_gather x4 -> x0, blocking collectives: 98.4 us -> none  [the longest x1 33.5 us: body(): lax.all_gather(col_bw, 'col', axis=0, tiled=True)]
    reduce_scatter x1 -> x0, waiting for transfers between devices: 55 us -> none  [body(): lax.psum_scatter(mixed_sums.reshape(COLS, cells_row), 'col', scatter_dime...]
    gather x98 -> x0, local copies, waits for them, and re-layouts: 54.9 us -> none  [the longest x14 8 us: block_kernel(): right_prof = jnp.take(col_prof, col_slots, axis=1)]
    dot_general x41 -> x0, matrix products: 25.3 us -> none  [the longest x12 9.16 us: block_kernel(): jnp.einsum('pkb,pkd->kbd', left_prof, right_prof, preferred_element_type=...]
    all_gather x1 -> x0, waiting for transfers between devices: 18.9 us -> none  [body(): lax.all_gather(col_prof, 'col', axis=1, tiled=True)]
  transfers between devices with their start and end apart: 2 -> 0, of which waited for: 2 -> 0; matrix products, arithmetic and copies ran while one was open for 1% -> 0% of each run, Pallas kernels for 0% -> 0%
where the time goes in v1:
time: 180 us
  Pallas kernels  174 us (97%)
  between operations  2.03 us (1%)
  local copies, waits for them, and re-layouts  1.94 us (1%)
    pallas_call x1, Pallas kernels, body(): pl.pallas_call(functools.partial(tile_kernel, (NR, NC, NX, NY, slots)), o...  167 us
    pallas_call x1, Pallas kernels, body(): pl.pallas_call(functools.partial(finish_kernel, cells=landmarks.shape[0]...  7.56 us

profile of v1, /device:TPU:1, one launch (start us, length us, event | category | flops | bytes accessed | tf_op | source)
XLA Modules:
  0.0 179.7 jit_solution(9226877656301498912)
XLA Ops:
  1.3 0.0 copy-start.1
  1.3 0.6 copy-done.1
  1.9 0.6 compare_reduce_fusion
  3.2 0.0 copy-start
  3.2 0.7 copy-done
  3.9 0.2 convert_reduce_fusion.1
  4.1 0.1 select_reduce_fusion
  4.3 0.1 fusion
  4.4 0.1 convert_reduce_fusion
  4.6 0.1 compare_convert_fusion
  4.6 0.6 stack.16.idx
  5.2 166.9 %tile.1 = (f32[32,128]{1,0:T(8,128)}, f32[64,128]{1,0:T(8,128)}, f32[32,128]{1,0:T(8,128)}, f32[16,128]{1,0:T(8,128)}) custom-call(bf16[50,128]{1,0:T(8,128)(2,1)} %prof_ref.1, bf16[1,128]{1,0:T(2,128)(2,1)} %bitcast.29, bf16[64,128]{1,0:T(8,128)(2,1)} %basis_ref.1, s32[8,128]{1,0:T(8,128)} %stack.16.idx), custom_call_target="tpu_custom_call" | custom-call | tf_op jit(solution)/shard_map/tile/pallas_call | solution.py:427
  172.1 7.6 %finish.1 = (f32[64,128]{1,0:T(8,128)}, f32[32,128]{1,0:T(8,128)}, f32[16,128]{1,0:T(8,128)}) custom-call(f32[32,128]{1,0:T(8,128)} %get-tuple-element.10.gram_ref, f32[64,128]{1,0:T(8,128)} %get-tuple-element.11.proj_ref, f32[32,128]{1,0:T(8,128)} %get-tuple-element.12.rows_in, f32[16,128]{1,0:T(8,128)} %get-tuple-element.13.cols_in), custom_call_target="tpu_custom_call" | custom-call | tf_op jit(solution)/shard_map/finish/pallas_call | solution.py:470
  (9 shorter events, 0.0 us)
Async XLA Ops:
  1.3 0.7 copy-start.1
  3.2 0.7 copy-start

commit v2 on v1

--- a/solution.py
+++ b/solution.py
@@ -63,20 +63,20 @@
     left,
     uleft,
     uright,
-    hot16,
-    hot32,
-    rhi,
-    rlo,
-    chi,
-    clo,
+    hot,
+    rsplit,
+    csplit,
     sbas,
     aff,
     sums,
+    rowsums,
+    rowpick,
     share,
     zvec,
     xvec,
     yvec,
     xshare,
+    ysend,
     yshare,
     xgram,
     ygram,
@@ -104,6 +104,23 @@
     def ydev(d):
         return (me_r, me_x * NY + lax.rem(me_y + d, NY))
 
+    awaited = {}
+
+    def expect(region, number):
+        awaited[number] = region
+
+        def wait():
+            del awaited[number]
+            pltpu.make_async_copy(region, region, recv_sem.at[number]).wait()
+
+        return wait
+
+    def drain():
+        for number, region in list(awaited.items()):
+            pltpu.make_async_copy(region, region, recv_sem.at[number]).wait()
+        for region, number in sent:
+            pltpu.make_async_copy(region, region, send_sem.at[number]).wait()
+
     groups = {"z": (NR, zdev), "x": (NX, xdev), "y": (NY, ydev)}
     sent = []
 
@@ -120,7 +137,7 @@
             ).start()
         region = dst.at[pl.ds(1, size - 1)]
         sent.append((region, number))
-        return lambda: pltpu.make_async_copy(region, region, recv_sem.at[number]).wait()
+        return expect(region, number)
 
     prof = prof_ref[...].astype(f32)
     half = jnp.sum(prof * prof, axis=0, keepdims=True) * -0.5
@@ -157,20 +174,14 @@
 
     near = NR + NX + NY - 3
 
-    it16 = lax.broadcasted_iota(jnp.int32, (CP, BLK), 0)
-    it32 = lax.broadcasted_iota(jnp.int32, (RP, BLK), 0)
+    it = lax.broadcasted_iota(jnp.int32, (2 * CP, BLK), 0)
 
     def tables(k, carry):
-        hot32[k] = (it32 == k).astype(f32).astype(bf16)
+        hot[k] = ((it == k) | (it == k + CP)).astype(f32).astype(bf16)
         return carry
 
-    lax.fori_loop(0, RP + 1, tables, 0)
-
-    def tables16(k, carry):
-        hot16[k] = (it16 == k).astype(f32).astype(bf16)
-        return carry
-
-    lax.fori_loop(0, CP + 1, tables16, 0)
+    lax.fori_loop(0, CP, tables, 0)
+    hot[CP] = jnp.zeros((2 * CP, BLK), bf16)
 
     pl.semaphore_wait(barrier, near + 2 * moves.astype(jnp.int32))
 
@@ -203,38 +214,38 @@
     def _():
         stay.wait()
 
-    for d in range(1, NX):
+    for d in range(1, NY):
         pltpu.make_async_remote_copy(
             src_ref=rowbuf.at[0],
             dst_ref=rowbuf.at[d],
             send_sem=send_sem.at[2],
             recv_sem=recv_sem.at[2],
+            device_id=ydev(d),
+            device_id_type=MESH,
+        ).start()
+    region = rowbuf.at[pl.ds(1, NY - 1)]
+    sent.append((region, 2))
+    pltpu.make_async_copy(region, region, recv_sem.at[2]).wait()
+    for d in range(1, NX):
+        pltpu.make_async_remote_copy(
+            src_ref=rowbuf.at[pl.ds(0, NY)],
+            dst_ref=rowbuf.at[pl.ds(d * NY, NY)],
+            send_sem=send_sem.at[3],
+            recv_sem=recv_sem.at[3],
             device_id=xdev(d),
             device_id_type=MESH,
         ).start()
-    region = rowbuf.at[pl.ds(1, NX - 1)]
-    sent.append((region, 2))
-    pltpu.make_async_copy(region, region, recv_sem.at[2]).wait()
-    for d in range(1, NY):
-        pltpu.make_async_remote_copy(
-            src_ref=rowbuf.at[pl.ds(0, NX)],
-            dst_ref=rowbuf.at[pl.ds(d * NX, NX)],
-            send_sem=send_sem.at[3],
-            recv_sem=recv_sem.at[3],
-            device_id=ydev(d),
-            device_id_type=MESH,
-        ).start()
-    region_y = rowbuf.at[pl.ds(NX, (NY - 1) * NX)]
-    sent.append((region_y, 3))
-
-    wait_basis = push("z", lambda d: basisbuf.at[0], basisbuf, 4)
+    region_x = rowbuf.at[pl.ds(NY, (NX - 1) * NY)]
+    sent.append((region_x, 3))
+    wait_rows = expect(region_x, 3)
+
     wait_col()
 
     def col_place(j):
         return lax.rem(me_r - j + NR, NR)
 
     def row_place(i):
-        return lax.rem(me_y - lax.rem(i, NY) + NY, NY) * NX + lax.rem(me_x - i // NY + NX, NX)
+        return lax.rem(me_x - i // NY + NX, NX) * NY + lax.rem(me_y - lax.rem(i, NY) + NY, NY)
 
     def col_prepare(n, carry):
         turned = colbuf[n].astype(f32).T
@@ -245,7 +256,7 @@
 
     lax.fori_loop(0, NR, col_prepare, 0)
 
-    pltpu.make_async_copy(region_y, region_y, recv_sem.at[3]).wait()
+    wait_rows()
 
     def row_prepare(n, carry):
         w = rowbuf[n].astype(f32)[56:57, :]
@@ -254,37 +265,53 @@
 
     lax.fori_loop(0, NC, row_prepare, 0)
 
-    def build(s, carry):
-        j = col_place(idx[COL, s])
-        i = row_place(idx[ROW, s])
-        d = jnp.dot(left[j], rowbuf[i], preferred_element_type=f32)
-        e = d * uleft[j] * uright[i][0:1, :]
-        aff[s] = jnp.exp2(e).astype(bf16)
+    pairs = slots // 2
+
+    def build(p, carry):
+        for h in range(2):
+            j = col_place(idx[COL, 2 * p + h])
+            i = row_place(idx[ROW, 2 * p + h])
+            d = jnp.dot(left[j], rowbuf[i], preferred_element_type=f32)
+            e = d * uleft[j] * uright[i][0:1, :]
+            aff[p, :, h * BLK : (h + 1) * BLK] = jnp.exp2(e).astype(bf16)
         return carry
 
-    lax.fori_loop(0, slots, build, 0, unroll=4)
+    lax.fori_loop(0, pairs, build, 0, unroll=4)
 
     def col_pass():
-        def step(s, acc):
-            i = idx[ROW, s]
-            hot = hot16[idx[COLKEY, s]]
-            lhs = jnp.concatenate([rhi[i] * hot, rlo[i] * hot], axis=0)
+        def step(p, acc):
+            s, t = 2 * p, 2 * p + 1
+            lhs = jnp.concatenate(
+                [
+                    rsplit[idx[ROW, s]] * hot[idx[COLKEY, s]],
+                    rsplit[idx[ROW, t]] * hot[idx[COLKEY, t]],
+                ],
+                axis=1,
+            )
             return acc + lax.dot_general(
-                lhs, aff[s], (((1,), (1,)), ((), ())), preferred_element_type=f32
+                lhs, aff[p], (((1,), (1,)), ((), ())), preferred_element_type=f32
             )
 
-        acc = lax.fori_loop(0, slots, step, jnp.zeros((2 * CP, BLK), f32), unroll=4)
+        acc = lax.fori_loop(0, pairs, step, jnp.zeros((2 * CP, BLK), f32), unroll=8)
         return acc[0:CP] + acc[CP:]
 
+    sub8 = lax.broadcasted_iota(jnp.int32, (8, BLK), 0)
+
     def row_pass():
-        def step(s, acc):
-            j = idx[COL, s]
-            hot = hot32[idx[ROWKEY, s]]
-            lhs = jnp.concatenate([chi[j] * hot, clo[j] * hot], axis=0)
-            return acc + jnp.dot(lhs, aff[s], preferred_element_type=f32)
-
-        acc = lax.fori_loop(0, slots, step, jnp.zeros((2 * RP, BLK), f32), unroll=4)
-        return acc[0:RP] + acc[RP:]
+        def step(p, acc):
+            s, t = 2 * p, 2 * p + 1
+            lhs = csplit[idx[COL, s], 0] + csplit[idx[COL, t], 1]
+            both = jnp.dot(lhs, aff[p], preferred_element_type=f32)
+            acc = acc * idx[KEEP, s].astype(f32) + jnp.where(sub8 < 2, both[:, :BLK], 0.0)
+            rowsums[s] = acc
+            acc = acc * idx[KEEP, t].astype(f32) + jnp.where(sub8 < 2, 0.0, both[:, BLK:])
+            rowsums[t] = acc
+            return acc
+
+        lax.fori_loop(0, pairs, step, jnp.zeros((8, BLK), f32), unroll=8)
+        for i in range(NC):
+            rowpick[i] = rowsums[idx[LAST, i]] * idx[HAS, i].astype(f32)
+        return jnp.sum(rowpick[...], axis=1)
 
     def col_total(k, part):
         buf = zvec.at[k]
@@ -296,12 +323,10 @@
             total = total + buf[lax.rem(me_r - r + NR, NR)]
         return total
 
-    def row_total(k, part, during=None):
+    def row_total(k, part):
         bx = xvec.at[k]
         bx[0] = part
         wait = push("x", lambda d: bx.at[0], bx, 8 + k)
-        if during is not None:
-            during()
         wait()
         total = bx[me_x]
         for x in range(1, NX):
@@ -314,21 +339,36 @@
             total = total + by[lax.rem(me_y - y + NY, NY)]
         return total
 
-    def spread(vec, blocks, width_, hi_ref, lo_ref):
-        for n in range(blocks):
-            v = jnp.broadcast_to(vec[n : n + 1, :], (width_, BLK))
-            hi = v.astype(bf16)
-            hi_ref[n] = hi
-            lo_ref[n] = (v - hi.astype(f32)).astype(bf16)
-
-    rhi[...] = jnp.ones_like(rhi)
-    rlo[...] = jnp.zeros_like(rlo)
+    def split(v):
+        hi = v.astype(bf16).astype(f32)
+        return hi, v - hi
+
+    def spread_rows(vec):
+        for n in range(NC):
+            hi, lo = split(jnp.broadcast_to(vec[n : n + 1, :], (CP, BLK)))
+            rsplit[n] = jnp.concatenate([hi, lo], axis=0).astype(bf16)
+
+    def spread_cols(vec):
+        for n in range(NR):
+            hi, lo = split(jnp.broadcast_to(vec[n : n + 1, :], (8, BLK)))
+            even = jnp.where(sub8 % 2 == 0, hi, lo)
+            csplit[n, 0] = jnp.where(sub8 < 2, even, 0.0).astype(bf16)
+            csplit[n, 1] = jnp.where((sub8 >= 2) & (sub8 < 4), even, 0.0).astype(bf16)
+
+    first = lax.broadcasted_iota(jnp.int32, (NC, 2 * CP, BLK), 1)
+    rsplit[...] = jnp.where(first < CP, 1.0, 0.0).astype(bf16)
     for k in range(SWEEPS):
-        cvec = SCALE / col_total(k, col_pass())
-        spread(cvec, NR, RP, chi, clo)
+        part = col_pass()
+        cols_ref[...] = part
+        cvec = SCALE / col_total(k, part)
+        spread_cols(cvec)
         if k < SWEEPS - 1:
-            rvec = SCALE / row_total(k, row_pass())
-            spread(rvec, NC, CP, rhi, rlo)
+            part = row_pass()
+            rows_ref[...] = part
+            if k == 0:
+                wait_basis = push("z", lambda d: basisbuf.at[0], basisbuf, 4)
+            rvec = SCALE / row_total(k, part)
+            spread_rows(rvec)
     cols_ref[...] = cvec
 
     wait_basis()
@@ -336,41 +376,45 @@
         block = basisbuf[col_place(j)].astype(f32) * cvec[j : j + 1, :]
         sbas[j] = block.astype(bf16)
 
-    def subspace():
-        def step(s, acc):
-            keep = idx[KEEP, s].astype(f32)
-            acc = acc * keep + jnp.dot(sbas[idx[COL, s]], aff[s], preferred_element_type=f32)
+    def subspace(p, acc):
+        for h in range(2):
+            s = 2 * p + h
+            product = jnp.dot(
+                sbas[idx[COL, s]],
+                aff[p, :, h * BLK : (h + 1) * BLK],
+                preferred_element_type=f32,
+            )
+            acc = acc * idx[KEEP, s].astype(f32) + product
             sums[s] = acc
-            return acc
-
-        lax.fori_loop(0, slots, step, jnp.zeros((COLS, BLK), f32), unroll=4)
-
-        def pick(i, carry):
-            share[i] = sums[idx[LAST, i]] * idx[HAS, i].astype(f32)
-            return carry
-
-        lax.fori_loop(0, NC, pick, 0)
-
-    rvec = SCALE / row_total(SWEEPS - 1, row_pass(), subspace)
-    rows_ref[...] = rvec
+        return acc
+
+    lax.fori_loop(0, pairs, subspace, jnp.zeros((COLS, BLK), f32), unroll=4)
+
+    def pick(i, carry):
+        share[i] = (sums[idx[LAST, i]] * idx[HAS, i].astype(f32)).astype(share.dtype)
+        return carry
+
+    lax.fori_loop(0, NC, pick, 0)
 
     def own_part(x):
         return share.at[pl.ds(x * NY, NY)]
 
-    wait = push("x", lambda d: own_part(lax.rem(me_x + d, NX)), xshare, 14)
-    wait()
+    wait_share = push("x", lambda d: own_part(lax.rem(me_x + d, NX)), xshare, 14)
+    part = row_pass()
+    rvec = SCALE / row_total(SWEEPS - 1, part)
+    rows_ref[...] = rvec
+    wait_share()
 
     def add_x(n, carry):
-        total = jnp.zeros((COLS, BLK), f32) + share[me_x * NY + n]
+        total = share[me_x * NY + n].astype(f32)
         for d in range(1, NX):
-            total = total + xshare[d, n]
-        xshare[0, n] = total
+            total = total + xshare[d, n].astype(f32)
+        ysend[n] = total
         return carry
 
     lax.fori_loop(0, NY, add_x, 0)
-    wait = push("y", lambda d: xshare.at[0, lax.rem(me_y + d, NY)], yshare, 15)
-    wait()
-    total = xshare[0, me_y]
+    push("y", lambda d: ysend.at[lax.rem(me_y + d, NY)], yshare, 15)()
+    total = ysend[me_y]
     for d in range(1, NY):
         total = total + yshare[d]
     proj = total * (rows_ref[pl.ds(me_c, 1), :] * (1.0 / SCALE))
@@ -394,8 +438,7 @@
             packed = packed + buf[lax.rem(me - n + size, size)]
     gram_ref[...] = packed
 
-    for region, number in sent:
-        pltpu.make_async_copy(region, region, send_sem.at[number]).wait()
+    drain()
 
 
 def finish_kernel(gram_ref, proj_ref, rows_in, cols_in, ritz_ref, rows_ref, cols_ref, *, cells):
@@ -405,15 +448,21 @@
     packed = gram_ref[...] * (1.0 / cells)
     gram = jnp.concatenate([packed[:, :COLS], packed[:, COLS:]], axis=0)
     proj = proj_ref[...]
-    number = lax.broadcasted_iota(jnp.int32, (COLS, 1), 0)
+    gs = [gram[n : n + 8] for n in range(0, COLS, 8)]
+    ps = [proj[n : n + 8] for n in range(0, COLS, 8)]
     for k in range(COLS):
-        scale = 1.0 / jnp.sqrt(gram[k : k + 1, k : k + 1])
-        grow = gram[k : k + 1, :] * scale
-        prow = proj[k : k + 1, :] * scale
-        ritz_ref[k : k + 1, :] = prow
-        factor = jnp.where(number > k, gram[:, k : k + 1] * scale, 0.0)
-        gram = gram - factor * grow
-        proj = proj - factor * prow
+        top, row = k // 8, k % 8
+        cols = [jnp.broadcast_to(g[:, k : k + 1], (8, BLK)) for g in gs[top:]]
+        pivot = cols[0][row : row + 1, :]
+        inv = 1.0 / pivot
+        grow = gs[top][row : row + 1, :] * inv[:, :COLS]
+        prow = ps[top][row : row + 1, :]
+        ritz_ref[k : k + 1, :] = prow * (1.0 / jnp.sqrt(pivot))
+        prow = prow * inv
+        for n in range(top, COLS // 8):
+            col = cols[n - top]
+            gs[n] = gs[n] - col[:, :COLS] * grow
+            ps[n] = ps[n] - col * prow
 
 
 def body(mesh_sizes, profiles, cell_width, basis, block_lists, block_counts, landmarks):
@@ -429,7 +478,7 @@
         out_shape=(
             jax.ShapeDtypeStruct((half_rows, BLK), f32),
             jax.ShapeDtypeStruct((COLS, BLK), f32),
-            jax.ShapeDtypeStruct((RP, BLK), f32),
+            jax.ShapeDtypeStruct((NC, BLK), f32),
             jax.ShapeDtypeStruct((CP, BLK), f32),
         ),
         in_specs=[vmem, vmem, vmem, smem],
@@ -443,20 +492,20 @@
             pltpu.VMEM((NR, BLK, KDIM), bf16),
             pltpu.VMEM((NR, BLK, BLK), f32),
             pltpu.VMEM((NC, 8, BLK), f32),
-            pltpu.VMEM((CP + 1, CP, BLK), bf16),
-            pltpu.VMEM((RP + 1, RP, BLK), bf16),
-            pltpu.VMEM((NC, CP, BLK), bf16),
-            pltpu.VMEM((NC, CP, BLK), bf16),
-            pltpu.VMEM((NR, RP, BLK), bf16),
-            pltpu.VMEM((NR, RP, BLK), bf16),
+            pltpu.VMEM((CP + 1, 2 * CP, BLK), bf16),
+            pltpu.VMEM((NC, 2 * CP, BLK), bf16),
+            pltpu.VMEM((NR, 2, 8, BLK), bf16),
             pltpu.VMEM((NR, COLS, BLK), bf16),
-            pltpu.VMEM((slots, BLK, BLK), bf16),
+            pltpu.VMEM((slots // 2, BLK, 2 * BLK), bf16),
             pltpu.VMEM((slots, COLS, BLK), f32),
+            pltpu.VMEM((slots, 8, BLK), f32),
+            pltpu.VMEM((NC, 8, BLK), f32),
             pltpu.VMEM((NC, COLS, BLK), f32),
             pltpu.VMEM((SWEEPS, NR, CP, BLK), f32),
-            pltpu.VMEM((SWEEPS, NX, RP, BLK), f32),
-            pltpu.VMEM((SWEEPS, NY, RP, BLK), f32),
+            pltpu.VMEM((SWEEPS, NX, NC, BLK), f32),
+            pltpu.VMEM((SWEEPS, NY, NC, BLK), f32),
             pltpu.VMEM((NX, NY, COLS, BLK), f32),
+            pltpu.VMEM((NY, COLS, BLK), f32),
             pltpu.VMEM((NY, COLS, BLK), f32),
             pltpu.VMEM((NX, half_rows, BLK), f32),
             pltpu.VMEM((NY, half_rows, BLK), f32),
@@ -471,14 +520,14 @@
         functools.partial(finish_kernel, cells=landmarks.shape[0] * BLK),
         out_shape=(
             jax.ShapeDtypeStruct((COLS, BLK), f32),
-            jax.ShapeDtypeStruct((RP, BLK), f32),
+            jax.ShapeDtypeStruct((NC, BLK), f32),
             jax.ShapeDtypeStruct((CP, BLK), f32),
         ),
         in_specs=[vmem] * 4,
         out_specs=(vmem,) * 3,
         name="finish",
     )(gram, proj, rows, cols)
-    return rows[:NC].reshape(-1), cols[:NR].reshape(-1), ritz
+    return rows.reshape(-1), cols[:NR].reshape(-1), ritz
 
 
 def solution(mesh):

time: 180 us -> 149 us (0.83)
  Pallas kernels: 174 us -> 143 us
    pallas_call x1, Pallas kernels: 167 us -> 136 us  [body(): pl.pallas_call(functools.partial(tile_kernel, (NR, NC, NX, NY, slots)), o...]
where the time goes in v2:
time: 149 us; the launch traced here: 148 us
  Pallas kernels  143 us (96%)
  between operations  2.03 us (1%)
  local copies, waits for them, and re-layouts  1.94 us (1%)
    pallas_call x1, Pallas kernels, body(): pl.pallas_call(functools.partial(tile_kernel, (NR, NC, NX, NY, slots)), o...  136 us
    pallas_call x1, Pallas kernels, body(): pl.pallas_call(functools.partial(finish_kernel, cells=landmarks.shape[0]...  6.71 us

profile of v2, /device:TPU:1, one launch (start us, length us, event | category | flops | bytes accessed | tf_op | source)
XLA Modules:
  0.0 148.4 jit_solution(11756568500747963369)
XLA Ops:
  1.3 0.0 copy-start.1
  1.3 0.6 copy-done.1
  1.9 0.6 compare_reduce_fusion
  3.2 0.0 copy-start
  3.2 0.7 copy-done
  3.9 0.2 convert_reduce_fusion.1
  4.1 0.1 select_reduce_fusion
  4.3 0.1 fusion
  4.4 0.1 convert_reduce_fusion
  4.6 0.1 compare_convert_fusion
  4.6 0.6 stack.16.idx
  5.2 136.5 %tile.1 = (f32[32,128]{1,0:T(8,128)}, f32[64,128]{1,0:T(8,128)}, f32[32,128]{1,0:T(8,128)}, f32[16,128]{1,0:T(8,128)}) custom-call(bf16[50,128]{1,0:T(8,128)(2,1)} %prof_ref.1, bf16[1,128]{1,0:T(2,128)(2,1)} %bitcast.29, bf16[64,128]{1,0:T(8,128)(2,1)} %basis_ref.1, s32[8,128]{1,0:T(8,128)} %stack.16.idx), custom_call_target="tpu_custom_call" | custom-call | tf_op jit(solution)/shard_map/tile/pallas_call | solution.py:476
  141.7 6.7 %finish.1 = (f32[64,128]{1,0:T(8,128)}, f32[32,128]{1,0:T(8,128)}, f32[16,128]{1,0:T(8,128)}) custom-call(f32[32,128]{1,0:T(8,128)} %get-tuple-element.10.gram_ref, f32[64,128]{1,0:T(8,128)} %get-tuple-element.11.proj_ref, f32[32,128]{1,0:T(8,128)} %get-tuple-element.12.rows_in, f32[16,128]{1,0:T(8,128)} %get-tuple-element.13.cols_in), custom_call_target="tpu_custom_call" | custom-call | tf_op jit(solution)/shard_map/finish/pallas_call | solution.py:519
  (9 shorter events, 0.0 us)
Async XLA Ops:
  1.3 0.7 copy-start.1
  3.2 0.7 copy-start

commit v3 on v2

--- a/solution.py
+++ b/solution.py
@@ -20,29 +20,36 @@
 f32 = jnp.float32
 bf16 = jnp.bfloat16
 
-ROW, COL, ROWKEY, COLKEY, KEEP, LAST, HAS, MARK = range(8)
-
-
-def slot_table(slot_lists, count, landmarks, own_block, row_blocks):
-    slots = slot_lists.shape[1]
-    number = jnp.arange(slots, dtype=jnp.int32)
-    live = number < count
-    row = slot_lists[0]
-    col = slot_lists[1]
-    key = jnp.where(live, row, RP) * slots + number
-    rank = jnp.sum((key[None, :] < key[:, None]).astype(jnp.int32), axis=1)
-    place = (rank[None, :] == number[:, None]).astype(jnp.int32)
-    pick = lambda v: jnp.sum(place * v[None, :], axis=1)
-    rows, cols, lives = pick(row), pick(col), pick(live.astype(jnp.int32))
-    rowkey = jnp.where(lives > 0, rows, RP)
-    colkey = jnp.where(lives > 0, cols, CP)
-    before = jnp.concatenate([jnp.full((1,), -1, jnp.int32), rowkey[:-1]])
-    keep = (before == rowkey).astype(jnp.int32)
-    upto = jnp.sum((rowkey[None, :] <= number[:, None]).astype(jnp.int32), axis=1)
-    has = jnp.any(rowkey[None, :] == number[:, None], axis=1).astype(jnp.int32)
-    last = jnp.clip(upto - 1, 0, slots - 1)
-    mark = jnp.broadcast_to(jnp.any(landmarks == own_block).astype(jnp.int32), (slots,))
-    return jnp.stack([rows, cols, rowkey, colkey, keep, last, has, mark])
+ROW, COL, ROWKEY, COLKEY, KEEP, LAST, HAS = range(7)
+
+
+def slot_table(lists_ref, count, table_ref):
+    slots = lists_ref.shape[-1]
+    lane = lax.broadcasted_iota(jnp.int32, (1, slots), 1)
+    live = (lane < count).astype(jnp.int32)
+    packed = live * 1024 + lists_ref[0, 0, 0:1, :] * 32 + lists_ref[0, 0, 1:2, :]
+    down = jnp.broadcast_to(packed, (slots, slots)).T
+    number = lax.broadcasted_iota(jnp.int32, (slots, slots), 0)
+    across = lax.broadcasted_iota(jnp.int32, (slots, slots), 1)
+    unlive = lambda v: jnp.where(v >= 1024, (v >> 5) & 31, RP)
+    key_across = unlive(packed) * slots + lane
+    key_down = unlive(down) * slots + number
+    rank = jnp.sum((key_down < key_across).astype(jnp.int32), axis=0, keepdims=True)
+    place = jnp.broadcast_to(rank, (slots, slots)).T == across
+    order = jnp.sum(jnp.where(place, down, 0), axis=0, keepdims=True)
+    rowkey = unlive(order)
+    rows_down = unlive(down)
+    upto = jnp.sum((rows_down <= across).astype(jnp.int32), axis=0, keepdims=True)
+    here = jnp.sum((rows_down == across).astype(jnp.int32), axis=0, keepdims=True)
+    key8 = jnp.broadcast_to(rowkey, (8, slots))
+    before = jnp.where(lane == 0, -1, pltpu.roll(key8, 1, 1)[0:1])
+    table_ref[ROW : ROW + 1, :] = (order >> 5) & 31
+    table_ref[COL : COL + 1, :] = order & 31
+    table_ref[ROWKEY : ROWKEY + 1, :] = rowkey
+    table_ref[COLKEY : COLKEY + 1, :] = jnp.where(order >= 1024, order & 31, CP)
+    table_ref[KEEP : KEEP + 1, :] = (before == rowkey).astype(jnp.int32)
+    table_ref[LAST : LAST + 1, :] = jnp.maximum(upto - 1, 0)
+    table_ref[HAS : HAS + 1, :] = jnp.minimum(here, 1)
 
 
 def tile_kernel(
@@ -50,11 +57,15 @@
     prof_ref,
     width_ref,
     basis_ref,
-    idx,
+    lists_ref,
+    count_ref,
+    marks_ref,
     gram_ref,
     proj_ref,
     rows_ref,
     cols_ref,
+    table_ref,
+    idx,
     msg32,
     rowout,
     colbuf,
@@ -78,9 +89,11 @@
     xshare,
     ysend,
     yshare,
+    gparts,
+    zgram,
     xgram,
     ygram,
-    zgram,
+    zall,
     send_sem,
     recv_sem,
 ):
@@ -89,11 +102,11 @@
     me_c = lax.axis_index("col")
     me_x = me_c // NY
     me_y = me_c % NY
+    own_block = (me_c % 2) * NR + me_r
     to_r = me_c // 2
-    to_c = (me_c % 2) * NR + me_r
-    from_c = 2 * me_r + me_c // NR
-    from_r = me_c % NR
-    moves = (to_r != me_r) | (to_c != me_c)
+    to_x = own_block // NY
+    own_y = lax.rem(own_block, NY)
+    stays = (to_r == me_r) & (to_x == me_x)
 
     def zdev(d):
         return (lax.rem(me_r + d, NR), me_c)
@@ -116,6 +129,8 @@
         return wait
 
     def drain():
+        pl.when(stays)(lambda: moved(NY - 1))
+        pl.when(jnp.logical_not(stays))(lambda: moved(NY))
         for number, region in list(awaited.items()):
             pltpu.make_async_copy(region, region, recv_sem.at[number]).wait()
         for region, number in sent:
@@ -167,12 +182,16 @@
         for d in range(1, size):
             pl.semaphore_signal(barrier, inc=1, device_id=device(d), device_id_type=MESH)
 
-    @pl.when(moves)
-    def _():
-        pl.semaphore_signal(barrier, inc=1, device_id=(to_r, to_c), device_id_type=MESH)
-        pl.semaphore_signal(barrier, inc=1, device_id=(from_r, from_c), device_id_type=MESH)
+    for n in range(NY):
+        block = me_x * NY + n
+        source = (lax.rem(block, NR), 2 * me_r + block // NR)
+
+        @pl.when((source[0] != me_r) | (source[1] != me_c))
+        def _(source=source):
+            pl.semaphore_signal(barrier, inc=1, device_id=source, device_id_type=MESH)
 
     near = NR + NX + NY - 3
+    far = NY - stays.astype(jnp.int32)
 
     it = lax.broadcasted_iota(jnp.int32, (2 * CP, BLK), 0)
 
@@ -183,49 +202,37 @@
     lax.fori_loop(0, CP, tables, 0)
     hot[CP] = jnp.zeros((2 * CP, BLK), bf16)
 
-    pl.semaphore_wait(barrier, near + 2 * moves.astype(jnp.int32))
-
-    move = pltpu.make_async_remote_copy(
-        src_ref=outgoing,
-        dst_ref=rowbuf.at[0],
-        send_sem=send_sem.at[0],
-        recv_sem=recv_sem.at[0],
-        device_id=(to_r, to_c),
-        device_id_type=MESH,
-    )
-    stay = pltpu.make_async_copy(outgoing, rowbuf.at[0], recv_sem.at[0])
-
-    @pl.when(moves)
-    def _():
-        move.start()
-
-    @pl.when(jnp.logical_not(moves))
-    def _():
-        stay.start()
+    slot_table(lists_ref, count_ref[0, 0], table_ref)
+    tabled = pltpu.make_async_copy(table_ref, idx, recv_sem.at[20])
+    tabled.start()
+    pl.semaphore_wait(barrier, near + far)
+
+    for n in range(NY):
+        here = stays & (me_y == n)
+
+        @pl.when(jnp.logical_not(here))
+        def _(n=n):
+            pltpu.make_async_remote_copy(
+                src_ref=rowout.at[0],
+                dst_ref=rowbuf.at[own_y],
+                send_sem=send_sem.at[0],
+                recv_sem=recv_sem.at[0],
+                device_id=(to_r, to_x * NY + n),
+                device_id_type=MESH,
+            ).start()
+
+        @pl.when(here)
+        def _():
+            pltpu.make_async_copy(rowout.at[0], rowbuf.at[own_y], recv_sem.at[0]).start()
 
     wait_col = push("z", lambda d: colbuf.at[0], colbuf, 1)
-
-    @pl.when(moves)
-    def _():
-        move.wait_recv()
-        move.wait_send()
-
-    @pl.when(jnp.logical_not(moves))
-    def _():
-        stay.wait()
-
-    for d in range(1, NY):
-        pltpu.make_async_remote_copy(
-            src_ref=rowbuf.at[0],
-            dst_ref=rowbuf.at[d],
-            send_sem=send_sem.at[2],
-            recv_sem=recv_sem.at[2],
-            device_id=ydev(d),
-            device_id_type=MESH,
-        ).start()
-    region = rowbuf.at[pl.ds(1, NY - 1)]
-    sent.append((region, 2))
-    pltpu.make_async_copy(region, region, recv_sem.at[2]).wait()
+    own_rows = rowbuf.at[pl.ds(0, NY)]
+    pltpu.make_async_copy(own_rows, own_rows, recv_sem.at[0]).wait()
+
+    def moved(blocks):
+        region = rowbuf.at[pl.ds(0, blocks)]
+        pltpu.make_async_copy(region, region, send_sem.at[0]).wait()
+
     for d in range(1, NX):
         pltpu.make_async_remote_copy(
             src_ref=rowbuf.at[pl.ds(0, NY)],
@@ -245,7 +252,7 @@
         return lax.rem(me_r - j + NR, NR)
 
     def row_place(i):
-        return lax.rem(me_x - i // NY + NX, NX) * NY + lax.rem(me_y - lax.rem(i, NY) + NY, NY)
+        return lax.rem(me_x - i // NY + NX, NX) * NY + lax.rem(i, NY)
 
     def col_prepare(n, carry):
         turned = colbuf[n].astype(f32).T
@@ -264,6 +271,8 @@
         return carry
 
     lax.fori_loop(0, NC, row_prepare, 0)
+
+    tabled.wait()
 
     pairs = slots // 2
 
@@ -323,21 +332,36 @@
             total = total + buf[lax.rem(me_r - r + NR, NR)]
         return total
 
-    def row_total(k, part):
+    def row_over_x(k, part):
         bx = xvec.at[k]
         bx[0] = part
         wait = push("x", lambda d: bx.at[0], bx, 8 + k)
-        wait()
-        total = bx[me_x]
-        for x in range(1, NX):
-            total = total + bx[lax.rem(me_x - x + NX, NX)]
+
+        def finish():
+            wait()
+            total = bx[me_x]
+            for x in range(1, NX):
+                total = total + bx[lax.rem(me_x - x + NX, NX)]
+            return total
+
+        return finish
+
+    def row_over_y(k, part):
         by = yvec.at[k]
-        by[0] = total
-        push("y", lambda d: by.at[0], by, 11 + k)()
-        total = by[me_y]
-        for y in range(1, NY):
-            total = total + by[lax.rem(me_y - y + NY, NY)]
-        return total
+        by[0] = part
+        wait = push("y", lambda d: by.at[0], by, 11 + k)
+
+        def finish():
+            wait()
+            total = by[me_y]
+            for y in range(1, NY):
+                total = total + by[lax.rem(me_y - y + NY, NY)]
+            return total
+
+        return finish
+
+    def row_total(k, part):
+        return row_over_y(k, row_over_x(k, part)())()
 
     def split(v):
         hi = v.astype(bf16).astype(f32)
@@ -371,6 +395,7 @@
             spread_rows(rvec)
     cols_ref[...] = cvec
 
+    over_x = row_over_x(SWEEPS - 1, row_pass())
     wait_basis()
     for j in range(NR):
         block = basisbuf[col_place(j)].astype(f32) * cvec[j : j + 1, :]
@@ -399,9 +424,9 @@
     def own_part(x):
         return share.at[pl.ds(x * NY, NY)]
 
+    over_y = row_over_y(SWEEPS - 1, over_x())
     wait_share = push("x", lambda d: own_part(lax.rem(me_x + d, NX)), xshare, 14)
-    part = row_pass()
-    rvec = SCALE / row_total(SWEEPS - 1, part)
+    rvec = SCALE / over_y()
     rows_ref[...] = rvec
     wait_share()
 
@@ -420,24 +445,37 @@
     proj = total * (rows_ref[pl.ds(me_c, 1), :] * (1.0 / SCALE))
     proj_ref[...] = proj
 
-    masked = proj * idx[MARK, 0].astype(f32)
+    cells = me_r * NC + me_c
+    mark = jnp.int32(0)
+    for n in range(marks_ref.shape[0]):
+        mark = mark + (marks_ref[n] == cells).astype(jnp.int32)
+    masked = proj * mark.astype(f32)
     gram = lax.dot_general(
         masked, masked, (((1,), (1,)), ((), ())), precision=highest, preferred_element_type=f32
     )
     half_rows = COLS // 2
     packed = jnp.concatenate([gram[:half_rows], gram[half_rows:]], axis=1)
+    part_rows = half_rows // NR
+    for n in range(NR):
+        gparts[n] = packed[n * part_rows : (n + 1) * part_rows]
+    zgram[0] = gparts[me_r]
+    push("z", lambda d: gparts.at[lax.rem(me_r + d, NR)], zgram, 16)()
+    total = zgram[me_r]
+    for n in range(1, NR):
+        total = total + zgram[lax.rem(me_r - n + NR, NR)]
     for axis, buf, number, size, me in (
-        ("x", xgram, 16, NX, me_x),
-        ("y", ygram, 17, NY, me_y),
-        ("z", zgram, 18, NR, me_r),
+        ("x", xgram, 17, NX, me_x),
+        ("y", ygram, 18, NY, me_y),
     ):
-        buf[0] = packed
+        buf[0] = total
         push(axis, lambda d, buf=buf: buf.at[0], buf, number)()
-        packed = buf[me]
+        total = buf[me]
         for n in range(1, size):
-            packed = packed + buf[lax.rem(me - n + size, size)]
-    gram_ref[...] = packed
-
+            total = total + buf[lax.rem(me - n + size, size)]
+    zall[0] = total
+    push("z", lambda d: zall.at[0], zall, 19)()
+    for n in range(NR):
+        gram_ref[n * part_rows : (n + 1) * part_rows, :] = zall[lax.rem(me_r - n + NR, NR)]
     drain()
 
 
@@ -450,26 +488,44 @@
     proj = proj_ref[...]
     gs = [gram[n : n + 8] for n in range(0, COLS, 8)]
     ps = [proj[n : n + 8] for n in range(0, COLS, 8)]
-    for k in range(COLS):
+    wide = 4
+    for k in range(0, COLS, wide):
         top, row = k // 8, k % 8
-        cols = [jnp.broadcast_to(g[:, k : k + 1], (8, BLK)) for g in gs[top:]]
-        pivot = cols[0][row : row + 1, :]
-        inv = 1.0 / pivot
-        grow = gs[top][row : row + 1, :] * inv[:, :COLS]
-        prow = ps[top][row : row + 1, :]
-        ritz_ref[k : k + 1, :] = prow * (1.0 / jnp.sqrt(pivot))
-        prow = prow * inv
+        cols = [
+            [jnp.broadcast_to(g[:, k + m : k + m + 1], (8, BLK)) for g in gs[top:]]
+            for m in range(wide)
+        ]
+        flat = lambda v, i: jnp.broadcast_to(v[row + i : row + i + 1, :], (8, v.shape[1]))
+        d = [[flat(cols[m][0], i) for m in range(wide)] for i in range(wide)]
+        grow = [flat(gs[top], i) for i in range(wide)]
+        prow = [flat(ps[top], i) for i in range(wide)]
+        inv = []
+        for i in range(wide):
+            inv.append(1.0 / d[i][i])
+            for j in range(i + 1, wide):
+                factor = d[j][i] * inv[i]
+                for m in range(j, wide):
+                    d[j][m] = d[j][m] - factor * d[i][m]
+                    d[m][j] = d[j][m]
+                grow[j] = grow[j] - factor[:, :COLS] * grow[i]
+                prow[j] = prow[j] - factor * prow[i]
+                cols[j] = [a - factor * b for a, b in zip(cols[j], cols[i])]
+        for i in range(wide):
+            scale = 1.0 / jnp.sqrt(d[i][i][0:1])
+            ritz_ref[k + i : k + i + 1, :] = prow[i][0:1] * scale
+        for i in range(wide):
+            grow[i] = grow[i] * inv[i][:, :COLS]
+            prow[i] = prow[i] * inv[i]
         for n in range(top, COLS // 8):
-            col = cols[n - top]
-            gs[n] = gs[n] - col[:, :COLS] * grow
-            ps[n] = ps[n] - col * prow
+            for i in range(wide):
+                col = cols[i][n - top]
+                gs[n] = gs[n] - col[:, :COLS] * grow[i]
+                ps[n] = ps[n] - col * prow[i]
 
 
 def body(mesh_sizes, profiles, cell_width, basis, block_lists, block_counts, landmarks):
     NR, NC, NX, NY = mesh_sizes
     slots = block_lists.shape[-1]
-    own_block = lax.axis_index("row") * NC + lax.axis_index("col")
-    table = slot_table(block_lists[0, 0], block_counts[0, 0], landmarks, own_block, NC)
     vmem = pl.BlockSpec(memory_space=pltpu.VMEM)
     smem = pl.BlockSpec(memory_space=pltpu.SMEM)
     half_rows = COLS // 2
@@ -481,9 +537,11 @@
             jax.ShapeDtypeStruct((NC, BLK), f32),
             jax.ShapeDtypeStruct((CP, BLK), f32),
         ),
-        in_specs=[vmem, vmem, vmem, smem],
+        in_specs=[vmem, vmem, vmem, vmem, smem, smem],
         out_specs=(vmem,) * 4,
         scratch_shapes=[
+            pltpu.VMEM((8, slots), jnp.int32),
+            pltpu.SMEM((8, slots), jnp.int32),
             pltpu.VMEM((2, KDIM, BLK), f32),
             pltpu.VMEM((1, KDIM, BLK), bf16),
             pltpu.VMEM((NR, KDIM, BLK), bf16),
@@ -507,15 +565,17 @@
             pltpu.VMEM((NX, NY, COLS, BLK), f32),
             pltpu.VMEM((NY, COLS, BLK), f32),
             pltpu.VMEM((NY, COLS, BLK), f32),
-            pltpu.VMEM((NX, half_rows, BLK), f32),
-            pltpu.VMEM((NY, half_rows, BLK), f32),
-            pltpu.VMEM((NR, half_rows, BLK), f32),
-            pltpu.SemaphoreType.DMA((20,)),
-            pltpu.SemaphoreType.DMA((20,)),
+            pltpu.VMEM((NR, half_rows // NR, BLK), f32),
+            pltpu.VMEM((NR, half_rows // NR, BLK), f32),
+            pltpu.VMEM((NX, half_rows // NR, BLK), f32),
+            pltpu.VMEM((NY, half_rows // NR, BLK), f32),
+            pltpu.VMEM((NR, half_rows // NR, BLK), f32),
+            pltpu.SemaphoreType.DMA((21,)),
+            pltpu.SemaphoreType.DMA((21,)),
         ],
         compiler_params=pltpu.CompilerParams(collective_id=0, has_side_effects=True),
         name="tile",
-    )(profiles, cell_width.reshape(1, BLK), basis, table)
+    )(profiles, cell_width.reshape(1, BLK), basis, block_lists, block_counts, landmarks)
     ritz, rows, cols = pl.pallas_call(
         functools.partial(finish_kernel, cells=landmarks.shape[0] * BLK),
         out_shape=(

time: 149 us -> 140 us (0.940)
  Pallas kernels: 143 us -> 138 us
  local copies, waits for them, and re-layouts: 1.94 us -> 0 us
    pallas_call x1, Pallas kernels: 6.71 us -> 4.14 us  [body(): pl.pallas_call(functools.partial(finish_kernel, cells=landmarks.shape[0]...]
    pallas_call x1, Pallas kernels: 136 us -> 134 us  [body(): pl.pallas_call(functools.partial(tile_kernel, (NR, NC, NX, NY, slots)), o...]
where the time goes in v3:
time: 140 us
  Pallas kernels  138 us (99%)
    pallas_call x1, Pallas kernels, body(): pl.pallas_call(functools.partial(tile_kernel, (NR, NC, NX, NY, slots)), o...  134 us
    pallas_call x1, Pallas kernels, body(): pl.pallas_call(functools.partial(finish_kernel, cells=landmarks.shape[0]...  4.14 us

profile of v3, /device:TPU:1, one launch (start us, length us, event | category | flops | bytes accessed | tf_op | source)
XLA Modules:
  0.0 139.8 jit_solution(4860053796607993591)
XLA Ops:
  1.3 134.3 %tile.1 = (f32[32,128]{1,0:T(8,128)}, f32[64,128]{1,0:T(8,128)}, f32[32,128]{1,0:T(8,128)}, f32[16,128]{1,0:T(8,128)}) custom-call(bf16[50,128]{1,0:T(8,128)(2,1)} %prof_ref.1, bf16[1,128]{1,0:T(2,128)(2,1)} %bitcast.3, bf16[64,128]{1,0:T(8,128)(2,1)} %basis_ref.1, s32[1,1,2,128]{3,2,1,0:T(2,128)} %lists_ref.1, s32[1,1]{1,0:T(1,128)S(6)} %copy.9.count_ref, ...), custom_call_target="tpu_custom_call" | custom-call | tf_op jit(solution)/shard_map/tile/pallas_call | solution.py:532
  135.6 4.1 %finish.1 = (f32[64,128]{1,0:T(8,128)}, f32[32,128]{1,0:T(8,128)}, f32[16,128]{1,0:T(8,128)}) custom-call(f32[32,128]{1,0:T(8,128)} %get-tuple-element.10.gram_ref, f32[64,128]{1,0:T(8,128)} %get-tuple-element.11.proj_ref, f32[32,128]{1,0:T(8,128)} %get-tuple-element.12.rows_in, f32[16,128]{1,0:T(8,128)} %get-tuple-element.13.cols_in), custom_call_target="tpu_custom_call" | custom-call | tf_op jit(solution)/shard_map/finish/pallas_call | solution.py:579

commit v4 on v3

--- a/solution.py
+++ b/solution.py
@@ -89,6 +89,11 @@
     xshare,
     ysend,
     yshare,
+    rlast,
+    markx,
+    gotx,
+    marky,
+    goty,
     gparts,
     zgram,
     xgram,
@@ -202,9 +207,6 @@
     lax.fori_loop(0, CP, tables, 0)
     hot[CP] = jnp.zeros((2 * CP, BLK), bf16)
 
-    slot_table(lists_ref, count_ref[0, 0], table_ref)
-    tabled = pltpu.make_async_copy(table_ref, idx, recv_sem.at[20])
-    tabled.start()
     pl.semaphore_wait(barrier, near + far)
 
     for n in range(NY):
@@ -226,6 +228,10 @@
             pltpu.make_async_copy(rowout.at[0], rowbuf.at[own_y], recv_sem.at[0]).start()
 
     wait_col = push("z", lambda d: colbuf.at[0], colbuf, 1)
+    slot_table(lists_ref, count_ref[0, 0], table_ref)
+    tabled = pltpu.make_async_copy(table_ref, idx, recv_sem.at[20])
+    tabled.start()
+    tabled.wait()
     own_rows = rowbuf.at[pl.ds(0, NY)]
     pltpu.make_async_copy(own_rows, own_rows, recv_sem.at[0]).wait()
 
@@ -271,8 +277,6 @@
         return carry
 
     lax.fori_loop(0, NC, row_prepare, 0)
-
-    tabled.wait()
 
     pairs = slots // 2
 
@@ -416,43 +420,52 @@
     lax.fori_loop(0, pairs, subspace, jnp.zeros((COLS, BLK), f32), unroll=4)
 
     def pick(i, carry):
-        share[i] = (sums[idx[LAST, i]] * idx[HAS, i].astype(f32)).astype(share.dtype)
+        share[i] = sums[idx[LAST, i]] * idx[HAS, i].astype(f32)
         return carry
 
     lax.fori_loop(0, NC, pick, 0)
+
+    marked = [jnp.clip(marks_ref[2 * me_r + h] - me_r * NC, 0, NC - 1) for h in range(2)]
+    both = jnp.concatenate([share[n] for n in marked], axis=0).T
+    x_cells, y_cells = BLK // NX, BLK // NC
+    for x in range(NX):
+        markx[x] = both[x * x_cells : (x + 1) * x_cells]
+    wait_markx = push("x", lambda d: markx.at[lax.rem(me_x + d, NX)], gotx, 21)
+    over_y = row_over_y(SWEEPS - 1, over_x())
 
     def own_part(x):
         return share.at[pl.ds(x * NY, NY)]
 
-    over_y = row_over_y(SWEEPS - 1, over_x())
     wait_share = push("x", lambda d: own_part(lax.rem(me_x + d, NX)), xshare, 14)
+    wait_markx()
+    total = markx[me_x]
+    for d in range(1, NX):
+        total = total + gotx[d]
+    for y in range(NY):
+        marky[y] = total[y * y_cells : (y + 1) * y_cells]
+    wait_marky = push("y", lambda d: marky.at[lax.rem(me_y + d, NY)], goty, 22)
     rvec = SCALE / over_y()
     rows_ref[...] = rvec
-    wait_share()
-
-    def add_x(n, carry):
-        total = share[me_x * NY + n].astype(f32)
-        for d in range(1, NX):
-            total = total + xshare[d, n].astype(f32)
-        ysend[n] = total
-        return carry
-
-    lax.fori_loop(0, NY, add_x, 0)
-    push("y", lambda d: ysend.at[lax.rem(me_y + d, NY)], yshare, 15)()
-    total = ysend[me_y]
+    for n in range(NC):
+        rlast[n] = jnp.broadcast_to(rvec[n : n + 1, :], (max(8, y_cells), BLK))
+    first_cell = me_x * x_cells + me_y * y_cells
+    lanes = lax.broadcasted_iota(jnp.int32, (y_cells, BLK), 1)
+    own = lanes == first_cell + lax.broadcasted_iota(jnp.int32, (y_cells, BLK), 0)
+    scales = [
+        jnp.sum(jnp.where(own, rlast[n][0:y_cells], 0.0), axis=1, keepdims=True)
+        for n in marked
+    ]
+    wait_marky()
+    total = marky[me_y]
     for d in range(1, NY):
-        total = total + yshare[d]
-    proj = total * (rows_ref[pl.ds(me_c, 1), :] * (1.0 / SCALE))
-    proj_ref[...] = proj
-
-    cells = me_r * NC + me_c
-    mark = jnp.int32(0)
-    for n in range(marks_ref.shape[0]):
-        mark = mark + (marks_ref[n] == cells).astype(jnp.int32)
-    masked = proj * mark.astype(f32)
-    gram = lax.dot_general(
-        masked, masked, (((1,), (1,)), ((), ())), precision=highest, preferred_element_type=f32
-    )
+        total = total + goty[d]
+    masked = total * (jnp.where(lanes < COLS, scales[0], scales[1]) * (1.0 / SCALE))
+    gram = jnp.zeros((COLS, COLS), f32)
+    for h in range(2):
+        cells = masked[:, h * COLS : (h + 1) * COLS]
+        gram = gram + lax.dot_general(
+            cells, cells, (((0,), (0,)), ((), ())), precision=highest, preferred_element_type=f32
+        )
     half_rows = COLS // 2
     packed = jnp.concatenate([gram[:half_rows], gram[half_rows:]], axis=1)
     part_rows = half_rows // NR
@@ -463,17 +476,38 @@
     total = zgram[me_r]
     for n in range(1, NR):
         total = total + zgram[lax.rem(me_r - n + NR, NR)]
-    for axis, buf, number, size, me in (
-        ("x", xgram, 17, NX, me_x),
-        ("y", ygram, 18, NY, me_y),
-    ):
-        buf[0] = total
-        push(axis, lambda d, buf=buf: buf.at[0], buf, number)()
+
+    def over(axis, buf, number, value):
+        buf[0] = value
+        return push(axis, lambda d: buf.at[0], buf, number)
+
+    def added(buf, size, me):
         total = buf[me]
         for n in range(1, size):
             total = total + buf[lax.rem(me - n + size, size)]
-    zall[0] = total
-    push("z", lambda d: zall.at[0], zall, 19)()
+        return total
+
+    over("y", ygram, 18, total)()
+    wait_xgram = over("x", xgram, 17, added(ygram, NY, me_y))
+    wait_share()
+
+    def add_x(n, carry):
+        total = share[me_x * NY + n]
+        for d in range(1, NX):
+            total = total + xshare[d, n]
+        ysend[n] = total
+        return carry
+
+    lax.fori_loop(0, NY, add_x, 0)
+    wait_yshare = push("y", lambda d: ysend.at[lax.rem(me_y + d, NY)], yshare, 15)
+    wait_xgram()
+    wait_zall = over("z", zall, 19, added(xgram, NX, me_x))
+    wait_yshare()
+    total = ysend[me_y]
+    for d in range(1, NY):
+        total = total + yshare[d]
+    proj_ref[...] = total * (rows_ref[pl.ds(me_c, 1), :] * (1.0 / SCALE))
+    wait_zall()
     for n in range(NR):
         gram_ref[n * part_rows : (n + 1) * part_rows, :] = zall[lax.rem(me_r - n + NR, NR)]
     drain()
@@ -565,13 +599,18 @@
             pltpu.VMEM((NX, NY, COLS, BLK), f32),
             pltpu.VMEM((NY, COLS, BLK), f32),
             pltpu.VMEM((NY, COLS, BLK), f32),
+            pltpu.VMEM((NC, max(8, BLK // NC), BLK), f32),
+            pltpu.VMEM((NX, BLK // NX, BLK), f32),
+            pltpu.VMEM((NX, BLK // NX, BLK), f32),
+            pltpu.VMEM((NY, BLK // NC, BLK), f32),
+            pltpu.VMEM((NY, BLK // NC, BLK), f32),
             pltpu.VMEM((NR, half_rows // NR, BLK), f32),
             pltpu.VMEM((NR, half_rows // NR, BLK), f32),
             pltpu.VMEM((NX, half_rows // NR, BLK), f32),
             pltpu.VMEM((NY, half_rows // NR, BLK), f32),
             pltpu.VMEM((NR, half_rows // NR, BLK), f32),
-            pltpu.SemaphoreType.DMA((21,)),
-            pltpu.SemaphoreType.DMA((21,)),
+            pltpu.SemaphoreType.DMA((23,)),
+            pltpu.SemaphoreType.DMA((23,)),
         ],
         compiler_params=pltpu.CompilerParams(collective_id=0, has_side_effects=True),
         name="tile",

time: 140 us -> 130 us (0.929)
  Pallas kernels: 138 us -> 129 us
    pallas_call x1, Pallas kernels: 134 us -> 125 us  [body(): pl.pallas_call(functools.partial(tile_kernel, (NR, NC, NX, NY, slots)), o...]
where the time goes in v4:
time: 130 us
  Pallas kernels  129 us (99%)
    pallas_call x1, Pallas kernels, body(): pl.pallas_call(functools.partial(tile_kernel, (NR, NC, NX, NY, slots)), o...  125 us
    pallas_call x1, Pallas kernels, body(): pl.pallas_call(functools.partial(finish_kernel, cells=landmarks.shape[0]...  4.14 us

profile of v4, /device:TPU:1, one launch (start us, length us, event | category | flops | bytes accessed | tf_op | source)
XLA Modules:
  0.0 130.0 jit_solution(11547036945962447520)
XLA Ops:
  1.3 124.5 %tile.1 = (f32[32,128]{1,0:T(8,128)}, f32[64,128]{1,0:T(8,128)}, f32[32,128]{1,0:T(8,128)}, f32[16,128]{1,0:T(8,128)}) custom-call(bf16[50,128]{1,0:T(8,128)(2,1)} %prof_ref.1, bf16[1,128]{1,0:T(2,128)(2,1)} %bitcast.3, bf16[64,128]{1,0:T(8,128)(2,1)} %basis_ref.1, s32[1,1,2,128]{3,2,1,0:T(2,128)} %lists_ref.1, s32[1,1]{1,0:T(1,128)S(6)} %copy.9.count_ref, ...), custom_call_target="tpu_custom_call" | custom-call | tf_op jit(solution)/shard_map/tile/pallas_call | solution.py:566
  125.8 4.1 %finish.1 = (f32[64,128]{1,0:T(8,128)}, f32[32,128]{1,0:T(8,128)}, f32[16,128]{1,0:T(8,128)}) custom-call(f32[32,128]{1,0:T(8,128)} %get-tuple-element.10.gram_ref, f32[64,128]{1,0:T(8,128)} %get-tuple-element.11.proj_ref, f32[32,128]{1,0:T(8,128)} %get-tuple-element.12.rows_in, f32[16,128]{1,0:T(8,128)} %get-tuple-element.13.cols_in), custom_call_target="tpu_custom_call" | custom-call | tf_op jit(solution)/shard_map/finish/pallas_call | solution.py:618

commit v5 on v4

--- a/solution.py
+++ b/solution.py
@@ -21,6 +21,10 @@
 bf16 = jnp.bfloat16
 
 ROW, COL, ROWKEY, COLKEY, KEEP, LAST, HAS = range(7)
+
+
+def far_first(size):
+    return sorted(range(1, size), key=lambda d: abs(2 * d - size))
 
 
 def slot_table(lists_ref, count, table_ref):
@@ -54,16 +58,20 @@
 
 def tile_kernel(
     dims,
-    prof_ref,
-    width_ref,
-    basis_ref,
-    lists_ref,
+    prof_hbm,
+    width_hbm,
+    basis_hbm,
+    lists_hbm,
     count_ref,
     marks_ref,
     gram_ref,
     proj_ref,
     rows_ref,
     cols_ref,
+    prof_ref,
+    width_ref,
+    lists_ref,
+    input_sem,
     table_ref,
     idx,
     msg32,
@@ -146,7 +154,7 @@
 
     def push(axis, src_of, dst, number):
         size, device = groups[axis]
-        for d in range(1, size):
+        for d in far_first(size):
             pltpu.make_async_remote_copy(
                 src_ref=src_of(d),
                 dst_ref=dst.at[d],
@@ -158,6 +166,33 @@
         region = dst.at[pl.ds(1, size - 1)]
         sent.append((region, number))
         return expect(region, number)
+
+    inputs = [
+        pltpu.make_async_copy(src, dst, input_sem.at[n])
+        for n, (src, dst) in enumerate(
+            (
+                (prof_hbm, prof_ref),
+                (width_hbm, width_ref),
+                (lists_hbm, lists_ref),
+                (basis_hbm, basisbuf.at[0]),
+            )
+        )
+    ]
+    for copy in inputs:
+        copy.start()
+    barrier = pltpu.get_barrier_semaphore()
+    for size, device in groups.values():
+        for d in far_first(size):
+            pl.semaphore_signal(barrier, inc=1, device_id=device(d), device_id_type=MESH)
+    for n in range(NY):
+        block = me_x * NY + n
+        source = (lax.rem(block, NR), 2 * me_r + block // NR)
+
+        @pl.when((source[0] != me_r) | (source[1] != me_c))
+        def _(source=source):
+            pl.semaphore_signal(barrier, inc=1, device_id=source, device_id_type=MESH)
+    for copy in inputs:
+        copy.wait()
 
     prof = prof_ref[...].astype(f32)
     half = jnp.sum(prof * prof, axis=0, keepdims=True) * -0.5
@@ -178,22 +213,8 @@
         w = 56 + side
         msg32[side, w : w + 1, :] = width
     colbuf[0] = msg32[1].astype(bf16)
-    basisbuf[0] = basis_ref[...]
     outgoing = rowout.at[0]
     rowout[0] = msg32[0].astype(bf16)
-
-    barrier = pltpu.get_barrier_semaphore()
-    for size, device in groups.values():
-        for d in range(1, size):
-            pl.semaphore_signal(barrier, inc=1, device_id=device(d), device_id_type=MESH)
-
-    for n in range(NY):
-        block = me_x * NY + n
-        source = (lax.rem(block, NR), 2 * me_r + block // NR)
-
-        @pl.when((source[0] != me_r) | (source[1] != me_c))
-        def _(source=source):
-            pl.semaphore_signal(barrier, inc=1, device_id=source, device_id_type=MESH)
 
     near = NR + NX + NY - 3
     far = NY - stays.astype(jnp.int32)
@@ -239,7 +260,7 @@
         region = rowbuf.at[pl.ds(0, blocks)]
         pltpu.make_async_copy(region, region, send_sem.at[0]).wait()
 
-    for d in range(1, NX):
+    for d in far_first(NX):
         pltpu.make_async_remote_copy(
             src_ref=rowbuf.at[pl.ds(0, NY)],
             dst_ref=rowbuf.at[pl.ds(d * NY, NY)],
@@ -289,7 +310,7 @@
             aff[p, :, h * BLK : (h + 1) * BLK] = jnp.exp2(e).astype(bf16)
         return carry
 
-    lax.fori_loop(0, pairs, build, 0, unroll=4)
+    lax.fori_loop(0, pairs, build, 0, unroll=8)
 
     def col_pass():
         def step(p, acc):
@@ -561,6 +582,7 @@
     NR, NC, NX, NY = mesh_sizes
     slots = block_lists.shape[-1]
     vmem = pl.BlockSpec(memory_space=pltpu.VMEM)
+    hbm = pl.BlockSpec(memory_space=pltpu.HBM)
     smem = pl.BlockSpec(memory_space=pltpu.SMEM)
     half_rows = COLS // 2
     gram, proj, rows, cols = pl.pallas_call(
@@ -571,9 +593,13 @@
             jax.ShapeDtypeStruct((NC, BLK), f32),
             jax.ShapeDtypeStruct((CP, BLK), f32),
         ),
-        in_specs=[vmem, vmem, vmem, vmem, smem, smem],
+        in_specs=[hbm, hbm, hbm, hbm, smem, smem],
         out_specs=(vmem,) * 4,
         scratch_shapes=[
+            pltpu.VMEM((PCS, BLK), bf16),
+            pltpu.VMEM((1, BLK), bf16),
+            pltpu.VMEM((1, 1, 2, slots), jnp.int32),
+            pltpu.SemaphoreType.DMA((4,)),
             pltpu.VMEM((8, slots), jnp.int32),
             pltpu.SMEM((8, slots), jnp.int32),
             pltpu.VMEM((2, KDIM, BLK), f32),

time: 130 us -> 125 us (0.962)
  Pallas kernels: 129 us -> 123 us
    pallas_call x1, Pallas kernels: 125 us -> 119 us  [body(): pl.pallas_call(functools.partial(tile_kernel, (NR, NC, NX, NY, slots)), o...]
where the time goes in v5:
time: 125 us
  Pallas kernels  123 us (98%)
  between operations  1.29 us (1%)
    pallas_call x1, Pallas kernels, body(): pl.pallas_call(functools.partial(tile_kernel, (NR, NC, NX, NY, slots)), o...  119 us
    pallas_call x1, Pallas kernels, body(): pl.pallas_call(functools.partial(finish_kernel, cells=landmarks.shape[0]...  4.14 us

profile of v5, /device:TPU:1, one launch (start us, length us, event | category | flops | bytes accessed | tf_op | source)
XLA Modules:
  0.0 124.5 jit_solution(7319046444895537360)
XLA Ops:
  1.3 119.1 %tile.1 = (f32[32,128]{1,0:T(8,128)}, f32[64,128]{1,0:T(8,128)}, f32[32,128]{1,0:T(8,128)}, f32[16,128]{1,0:T(8,128)}) custom-call(bf16[50,128]{1,0:T(8,128)(2,1)} %prof_hbm.1, bf16[1,128]{1,0:T(2,128)(2,1)} %bitcast.3, bf16[64,128]{1,0:T(8,128)(2,1)} %basis_hbm.1, s32[1,1,2,128]{3,2,1,0:T(2,128)} %lists_hbm.1, s32[1,1]{1,0:T(1,128)S(6)} %copy.9.count_ref, ...), custom_call_target="tpu_custom_call" | custom-call | tf_op jit(solution)/shard_map/tile/pallas_call | solution.py:588
  120.4 4.1 %finish.1 = (f32[64,128]{1,0:T(8,128)}, f32[32,128]{1,0:T(8,128)}, f32[16,128]{1,0:T(8,128)}) custom-call(f32[32,128]{1,0:T(8,128)} %get-tuple-element.10.gram_ref, f32[64,128]{1,0:T(8,128)} %get-tuple-element.11.proj_ref, f32[32,128]{1,0:T(8,128)} %get-tuple-element.12.rows_in, f32[16,128]{1,0:T(8,128)} %get-tuple-element.13.cols_in), custom_call_target="tpu_custom_call" | custom-call | tf_op jit(solution)/shard_map/finish/pallas_call | solution.py:644

commit v6 on v5

--- a/solution.py
+++ b/solution.py
@@ -94,18 +94,18 @@
     zvec,
     xvec,
     yvec,
+    zlast,
+    xlast,
+    ylast,
     xshare,
     ysend,
     yshare,
     rlast,
-    markx,
-    gotx,
-    marky,
-    goty,
+    marks,
+    gotmarks,
     gparts,
     zgram,
-    xgram,
-    ygram,
+    pgram,
     zall,
     send_sem,
     recv_sem,
@@ -149,12 +149,20 @@
         for region, number in sent:
             pltpu.make_async_copy(region, region, send_sem.at[number]).wait()
 
-    groups = {"z": (NR, zdev), "x": (NX, xdev), "y": (NY, ydev)}
+    def pdev(d):
+        return (me_r, lax.rem(me_c + d, NC))
+
+    def hops(d):
+        return min(d // NY, NX - d // NY) + min(d % NY, NY - d % NY)
+
+    groups = {"z": (NR, zdev), "x": (NX, xdev), "y": (NY, ydev), "p": (NC, pdev)}
+    steps = {axis: far_first(groups[axis][0]) for axis in "zxy"}
+    steps["p"] = sorted(range(1, NC), key=lambda d: -hops(d))
     sent = []
 
     def push(axis, src_of, dst, number):
         size, device = groups[axis]
-        for d in far_first(size):
+        for d in steps[axis]:
             pltpu.make_async_remote_copy(
                 src_ref=src_of(d),
                 dst_ref=dst.at[d],
@@ -181,9 +189,11 @@
     for copy in inputs:
         copy.start()
     barrier = pltpu.get_barrier_semaphore()
-    for size, device in groups.values():
-        for d in far_first(size):
-            pl.semaphore_signal(barrier, inc=1, device_id=device(d), device_id_type=MESH)
+    for axis in "pz":
+        for d in steps[axis]:
+            pl.semaphore_signal(
+                barrier, inc=1, device_id=groups[axis][1](d), device_id_type=MESH
+            )
     for n in range(NY):
         block = me_x * NY + n
         source = (lax.rem(block, NR), 2 * me_r + block // NR)
@@ -216,7 +226,7 @@
     outgoing = rowout.at[0]
     rowout[0] = msg32[0].astype(bf16)
 
-    near = NR + NX + NY - 3
+    near = NR + NC - 2
     far = NY - stays.astype(jnp.int32)
 
     it = lax.broadcasted_iota(jnp.int32, (2 * CP, BLK), 0)
@@ -348,39 +358,39 @@
         return jnp.sum(rowpick[...], axis=1)
 
     def col_total(k, part):
-        buf = zvec.at[k]
-        buf[0] = part
+        buf = zlast if k == SWEEPS - 1 else zvec.at[k]
+        buf[0] = part.astype(buf.dtype)
         wait = push("z", lambda d: buf.at[0], buf, 5 + k)
         wait()
-        total = buf[lax.rem(me_r, NR)]
+        total = buf[lax.rem(me_r, NR)].astype(f32)
         for r in range(1, NR):
-            total = total + buf[lax.rem(me_r - r + NR, NR)]
+            total = total + buf[lax.rem(me_r - r + NR, NR)].astype(f32)
         return total
 
     def row_over_x(k, part):
-        bx = xvec.at[k]
-        bx[0] = part
+        bx = xlast if k == SWEEPS - 1 else xvec.at[k]
+        bx[0] = part.astype(bx.dtype)
         wait = push("x", lambda d: bx.at[0], bx, 8 + k)
 
         def finish():
             wait()
-            total = bx[me_x]
+            total = bx[me_x].astype(f32)
             for x in range(1, NX):
-                total = total + bx[lax.rem(me_x - x + NX, NX)]
+                total = total + bx[lax.rem(me_x - x + NX, NX)].astype(f32)
             return total
 
         return finish
 
     def row_over_y(k, part):
-        by = yvec.at[k]
-        by[0] = part
+        by = ylast if k == SWEEPS - 1 else yvec.at[k]
+        by[0] = part.astype(by.dtype)
         wait = push("y", lambda d: by.at[0], by, 11 + k)
 
         def finish():
             wait()
-            total = by[me_y]
+            total = by[me_y].astype(f32)
             for y in range(1, NY):
-                total = total + by[lax.rem(me_y - y + NY, NY)]
+                total = total + by[lax.rem(me_y - y + NY, NY)].astype(f32)
             return total
 
         return finish
@@ -448,44 +458,35 @@
 
     marked = [jnp.clip(marks_ref[2 * me_r + h] - me_r * NC, 0, NC - 1) for h in range(2)]
     both = jnp.concatenate([share[n] for n in marked], axis=0).T
-    x_cells, y_cells = BLK // NX, BLK // NC
-    for x in range(NX):
-        markx[x] = both[x * x_cells : (x + 1) * x_cells]
-    wait_markx = push("x", lambda d: markx.at[lax.rem(me_x + d, NX)], gotx, 21)
+    cells = BLK // NC
+    for c in range(NC):
+        marks[c] = both[c * cells : (c + 1) * cells]
+    wait_marks = push("p", lambda d: marks.at[lax.rem(me_c + d, NC)], gotmarks, 21)
     over_y = row_over_y(SWEEPS - 1, over_x())
 
     def own_part(x):
         return share.at[pl.ds(x * NY, NY)]
 
     wait_share = push("x", lambda d: own_part(lax.rem(me_x + d, NX)), xshare, 14)
-    wait_markx()
-    total = markx[me_x]
-    for d in range(1, NX):
-        total = total + gotx[d]
-    for y in range(NY):
-        marky[y] = total[y * y_cells : (y + 1) * y_cells]
-    wait_marky = push("y", lambda d: marky.at[lax.rem(me_y + d, NY)], goty, 22)
     rvec = SCALE / over_y()
     rows_ref[...] = rvec
     for n in range(NC):
-        rlast[n] = jnp.broadcast_to(rvec[n : n + 1, :], (max(8, y_cells), BLK))
-    first_cell = me_x * x_cells + me_y * y_cells
-    lanes = lax.broadcasted_iota(jnp.int32, (y_cells, BLK), 1)
-    own = lanes == first_cell + lax.broadcasted_iota(jnp.int32, (y_cells, BLK), 0)
+        rlast[n] = jnp.broadcast_to(rvec[n : n + 1, :], (max(8, cells), BLK))
+    lanes = lax.broadcasted_iota(jnp.int32, (cells, BLK), 1)
+    own = lanes == me_c * cells + lax.broadcasted_iota(jnp.int32, (cells, BLK), 0)
     scales = [
-        jnp.sum(jnp.where(own, rlast[n][0:y_cells], 0.0), axis=1, keepdims=True)
-        for n in marked
+        jnp.sum(jnp.where(own, rlast[n][0:cells], 0.0), axis=1, keepdims=True) for n in marked
     ]
-    wait_marky()
-    total = marky[me_y]
-    for d in range(1, NY):
-        total = total + goty[d]
+    wait_marks()
+    total = marks[me_c]
+    for d in range(1, NC):
+        total = total + gotmarks[d]
     masked = total * (jnp.where(lanes < COLS, scales[0], scales[1]) * (1.0 / SCALE))
     gram = jnp.zeros((COLS, COLS), f32)
     for h in range(2):
-        cells = masked[:, h * COLS : (h + 1) * COLS]
+        block = masked[:, h * COLS : (h + 1) * COLS]
         gram = gram + lax.dot_general(
-            cells, cells, (((0,), (0,)), ((), ())), precision=highest, preferred_element_type=f32
+            block, block, (((0,), (0,)), ((), ())), precision=highest, preferred_element_type=f32
         )
     half_rows = COLS // 2
     packed = jnp.concatenate([gram[:half_rows], gram[half_rows:]], axis=1)
@@ -508,8 +509,7 @@
             total = total + buf[lax.rem(me - n + size, size)]
         return total
 
-    over("y", ygram, 18, total)()
-    wait_xgram = over("x", xgram, 17, added(ygram, NY, me_y))
+    wait_pgram = over("p", pgram, 17, total)
     wait_share()
 
     def add_x(n, carry):
@@ -521,8 +521,8 @@
 
     lax.fori_loop(0, NY, add_x, 0)
     wait_yshare = push("y", lambda d: ysend.at[lax.rem(me_y + d, NY)], yshare, 15)
-    wait_xgram()
-    wait_zall = over("z", zall, 19, added(xgram, NX, me_x))
+    wait_pgram()
+    wait_zall = over("z", zall, 19, added(pgram, NC, me_c))
     wait_yshare()
     total = ysend[me_y]
     for d in range(1, NY):
@@ -619,21 +619,21 @@
             pltpu.VMEM((slots, 8, BLK), f32),
             pltpu.VMEM((NC, 8, BLK), f32),
             pltpu.VMEM((NC, COLS, BLK), f32),
-            pltpu.VMEM((SWEEPS, NR, CP, BLK), f32),
-            pltpu.VMEM((SWEEPS, NX, NC, BLK), f32),
-            pltpu.VMEM((SWEEPS, NY, NC, BLK), f32),
+            pltpu.VMEM((SWEEPS - 1, NR, CP, BLK), bf16),
+            pltpu.VMEM((SWEEPS - 1, NX, NC, BLK), bf16),
+            pltpu.VMEM((SWEEPS - 1, NY, NC, BLK), bf16),
+            pltpu.VMEM((NR, CP, BLK), f32),
+            pltpu.VMEM((NX, NC, BLK), f32),
+            pltpu.VMEM((NY, NC, BLK), f32),
             pltpu.VMEM((NX, NY, COLS, BLK), f32),
             pltpu.VMEM((NY, COLS, BLK), f32),
             pltpu.VMEM((NY, COLS, BLK), f32),
             pltpu.VMEM((NC, max(8, BLK // NC), BLK), f32),
-            pltpu.VMEM((NX, BLK // NX, BLK), f32),
-            pltpu.VMEM((NX, BLK // NX, BLK), f32),
-            pltpu.VMEM((NY, BLK // NC, BLK), f32),
-            pltpu.VMEM((NY, BLK // NC, BLK), f32),
+            pltpu.VMEM((NC, BLK // NC, BLK), f32),
+            pltpu.VMEM((NC, BLK // NC, BLK), f32),
             pltpu.VMEM((NR, half_rows // NR, BLK), f32),
             pltpu.VMEM((NR, half_rows // NR, BLK), f32),
-            pltpu.VMEM((NX, half_rows // NR, BLK), f32),
-            pltpu.VMEM((NY, half_rows // NR, BLK), f32),
+            pltpu.VMEM((NC, half_rows // NR, BLK), f32),
             pltpu.VMEM((NR, half_rows // NR, BLK), f32),
             pltpu.SemaphoreType.DMA((23,)),
             pltpu.SemaphoreType.DMA((23,)),

time: 125 us -> 118 us (0.944)
  Pallas kernels: 123 us -> 116 us
    pallas_call x1, Pallas kernels: 119 us -> 112 us  [body(): pl.pallas_call(functools.partial(tile_kernel, (NR, NC, NX, NY, slots)), o...]
where the time goes in v6:
time: 118 us; the launch traced here: 117 us
  Pallas kernels  116 us (98%)
  between operations  1.29 us (1%)
    pallas_call x1, Pallas kernels, body(): pl.pallas_call(functools.partial(tile_kernel, (NR, NC, NX, NY, slots)), o...  112 us
    pallas_call x1, Pallas kernels, body(): pl.pallas_call(functools.partial(finish_kernel, cells=landmarks.shape[0]...  4.14 us

profile of v6, /device:TPU:1, one launch (start us, length us, event | category | flops | bytes accessed | tf_op | source)
XLA Modules:
  0.0 117.4 jit_solution(11247470271773412646)
XLA Ops:
  1.3 112.0 %tile.1 = (f32[32,128]{1,0:T(8,128)}, f32[64,128]{1,0:T(8,128)}, f32[32,128]{1,0:T(8,128)}, f32[16,128]{1,0:T(8,128)}) custom-call(bf16[50,128]{1,0:T(8,128)(2,1)} %prof_hbm.1, bf16[1,128]{1,0:T(2,128)(2,1)} %bitcast.3, bf16[64,128]{1,0:T(8,128)(2,1)} %basis_hbm.1, s32[1,1,2,128]{3,2,1,0:T(2,128)} %lists_hbm.1, s32[1,1]{1,0:T(1,128)S(6)} %copy.9.count_ref, ...), custom_call_target="tpu_custom_call" | custom-call | tf_op jit(solution)/shard_map/tile/pallas_call | solution.py:588
  113.2 4.1 %finish.1 = (f32[64,128]{1,0:T(8,128)}, f32[32,128]{1,0:T(8,128)}, f32[16,128]{1,0:T(8,128)}) custom-call(f32[32,128]{1,0:T(8,128)} %get-tuple-element.10.gram_ref, f32[64,128]{1,0:T(8,128)} %get-tuple-element.11.proj_ref, f32[32,128]{1,0:T(8,128)} %get-tuple-element.12.rows_in, f32[16,128]{1,0:T(8,128)} %get-tuple-element.13.cols_in), custom_call_target="tpu_custom_call" | custom-call | tf_op jit(solution)/shard_map/finish/pallas_call | solution.py:644

commit v7 on v6

--- a/solution.py
+++ b/solution.py
@@ -311,16 +311,23 @@
 
     pairs = slots // 2
 
-    def build(p, carry):
+    def build(p, acc):
+        halves = []
         for h in range(2):
             j = col_place(idx[COL, 2 * p + h])
             i = row_place(idx[ROW, 2 * p + h])
             d = jnp.dot(left[j], rowbuf[i], preferred_element_type=f32)
             e = d * uleft[j] * uright[i][0:1, :]
-            aff[p, :, h * BLK : (h + 1) * BLK] = jnp.exp2(e).astype(bf16)
-        return carry
-
-    lax.fori_loop(0, pairs, build, 0, unroll=8)
+            halves.append(jnp.exp2(e).astype(bf16))
+        block = jnp.concatenate(halves, axis=1)
+        aff[p] = block
+        keys = [idx[COLKEY, 2 * p + h] for h in range(2)]
+        lhs = jnp.concatenate([hot[k, 0:CP, :] for k in keys], axis=1)
+        return acc + lax.dot_general(
+            lhs, block, (((1,), (1,)), ((), ())), preferred_element_type=f32
+        )
+
+    first_part = lax.fori_loop(0, pairs, build, jnp.zeros((CP, BLK), f32), unroll=8)
 
     def col_pass():
         def step(p, acc):
@@ -414,10 +421,8 @@
             csplit[n, 0] = jnp.where(sub8 < 2, even, 0.0).astype(bf16)
             csplit[n, 1] = jnp.where((sub8 >= 2) & (sub8 < 4), even, 0.0).astype(bf16)
 
-    first = lax.broadcasted_iota(jnp.int32, (NC, 2 * CP, BLK), 1)
-    rsplit[...] = jnp.where(first < CP, 1.0, 0.0).astype(bf16)
     for k in range(SWEEPS):
-        part = col_pass()
+        part = first_part if k == 0 else col_pass()
         cols_ref[...] = part
         cvec = SCALE / col_total(k, part)
         spread_cols(cvec)

time: 118 us -> 117 us (level)
  no operation moved by 1% of the time
where the time goes in v7:
time: 117 us; the launch traced here: 116 us
  Pallas kernels  115 us (98%)
  between operations  1.29 us (1%)
    pallas_call x1, Pallas kernels, body(): pl.pallas_call(functools.partial(tile_kernel, (NR, NC, NX, NY, slots)), o...  111 us
    pallas_call x1, Pallas kernels, body(): pl.pallas_call(functools.partial(finish_kernel, cells=landmarks.shape[0]...  4.14 us

profile of v7, /device:TPU:1, one launch (start us, length us, event | category | flops | bytes accessed | tf_op | source)
XLA Modules:
  0.0 116.5 jit_solution(6762046887170267036)
XLA Ops:
  1.3 111.0 %tile.1 = (f32[32,128]{1,0:T(8,128)}, f32[64,128]{1,0:T(8,128)}, f32[32,128]{1,0:T(8,128)}, f32[16,128]{1,0:T(8,128)}) custom-call(bf16[50,128]{1,0:T(8,128)(2,1)} %prof_hbm.1, bf16[1,128]{1,0:T(2,128)(2,1)} %bitcast.3, bf16[64,128]{1,0:T(8,128)(2,1)} %basis_hbm.1, s32[1,1,2,128]{3,2,1,0:T(2,128)} %lists_hbm.1, s32[1,1]{1,0:T(1,128)S(6)} %copy.9.count_ref, ...), custom_call_target="tpu_custom_call" | custom-call | tf_op jit(solution)/shard_map/tile/pallas_call | solution.py:593
  112.3 4.1 %finish.1 = (f32[64,128]{1,0:T(8,128)}, f32[32,128]{1,0:T(8,128)}, f32[16,128]{1,0:T(8,128)}) custom-call(f32[32,128]{1,0:T(8,128)} %get-tuple-element.10.gram_ref, f32[64,128]{1,0:T(8,128)} %get-tuple-element.11.proj_ref, f32[32,128]{1,0:T(8,128)} %get-tuple-element.12.rows_in, f32[16,128]{1,0:T(8,128)} %get-tuple-element.13.cols_in), custom_call_target="tpu_custom_call" | custom-call | tf_op jit(solution)/shard_map/finish/pallas_call | solution.py:649

commit v8 on v7

--- a/solution.py
+++ b/solution.py
@@ -343,7 +343,7 @@
                 lhs, aff[p], (((1,), (1,)), ((), ())), preferred_element_type=f32
             )
 
-        acc = lax.fori_loop(0, pairs, step, jnp.zeros((2 * CP, BLK), f32), unroll=8)
+        acc = lax.fori_loop(0, pairs, step, jnp.zeros((2 * CP, BLK), f32), unroll=16)
         return acc[0:CP] + acc[CP:]
 
     sub8 = lax.broadcasted_iota(jnp.int32, (8, BLK), 0)
@@ -359,7 +359,7 @@
             rowsums[t] = acc
             return acc
 
-        lax.fori_loop(0, pairs, step, jnp.zeros((8, BLK), f32), unroll=8)
+        lax.fori_loop(0, pairs, step, jnp.zeros((8, BLK), f32), unroll=16)
         for i in range(NC):
             rowpick[i] = rowsums[idx[LAST, i]] * idx[HAS, i].astype(f32)
         return jnp.sum(rowpick[...], axis=1)

time: 117 us -> 115 us (0.983)
  Pallas kernels: 115 us -> 113 us
    pallas_call x1, Pallas kernels: 111 us -> 109 us  [body(): pl.pallas_call(functools.partial(tile_kernel, (NR, NC, NX, NY, slots)), o...]
where the time goes in v8:
time: 115 us
  Pallas kernels  113 us (98%)
  between operations  1.29 us (1%)
    pallas_call x1, Pallas kernels, body(): pl.pallas_call(functools.partial(tile_kernel, (NR, NC, NX, NY, slots)), o...  109 us
    pallas_call x1, Pallas kernels, body(): pl.pallas_call(functools.partial(finish_kernel, cells=landmarks.shape[0]...  4.14 us

profile of v8, /device:TPU:1, one launch (start us, length us, event | category | flops | bytes accessed | tf_op | source)
XLA Modules:
  0.0 114.5 jit_solution(17012505431919690070)
XLA Ops:
  1.3 109.1 %tile.1 = (f32[32,128]{1,0:T(8,128)}, f32[64,128]{1,0:T(8,128)}, f32[32,128]{1,0:T(8,128)}, f32[16,128]{1,0:T(8,128)}) custom-call(bf16[50,128]{1,0:T(8,128)(2,1)} %prof_hbm.1, bf16[1,128]{1,0:T(2,128)(2,1)} %bitcast.3, bf16[64,128]{1,0:T(8,128)(2,1)} %basis_hbm.1, s32[1,1,2,128]{3,2,1,0:T(2,128)} %lists_hbm.1, s32[1,1]{1,0:T(1,128)S(6)} %copy.9.count_ref, ...), custom_call_target="tpu_custom_call" | custom-call | tf_op jit(solution)/shard_map/tile/pallas_call | solution.py:593
  110.4 4.1 %finish.1 = (f32[64,128]{1,0:T(8,128)}, f32[32,128]{1,0:T(8,128)}, f32[16,128]{1,0:T(8,128)}) custom-call(f32[32,128]{1,0:T(8,128)} %get-tuple-element.10.gram_ref, f32[64,128]{1,0:T(8,128)} %get-tuple-element.11.proj_ref, f32[32,128]{1,0:T(8,128)} %get-tuple-element.12.rows_in, f32[16,128]{1,0:T(8,128)} %get-tuple-element.13.cols_in), custom_call_target="tpu_custom_call" | custom-call | tf_op jit(solution)/shard_map/finish/pallas_call | solution.py:649
